TPU v7x, 256 devices: a whole 4x4x8 slice. The times are simulated.
256 devices in a mesh: segment: 2 (over core), dom: 64 (over z, y, x_lo), rep: 2 (over x_hi).
Axes of the slice: x: 4 (x_hi: 2, x_lo: 2; x = x_hi * 2 + x_lo), y: 4, z: 8, core: 2. Of those that a mesh axis runs over, the one named last changes fastest.
Arguments:
- node_latent: bfloat16 [4, 8192, 512], P('rep', 'dom'), may hold values from -6 to 6
- edge_latent: bfloat16 [4, 24576, 512], P('rep', 'dom'), may hold values from -6 to 6
- node_cot: bfloat16 [4, 8192, 512], P('rep', 'dom'), may hold values from -6 to 6
- edge_src: int32 [24576], P('dom'), may hold values from 0 to 191, as said below
- edge_dst: int32 [24576], P('dom'), may hold values from 0 to 127
- edge_count: int32 [64], P('dom'), may hold values from 192 to 384, as said below
- send_index: int32 [64, 4, 16], P('dom'), may hold values from 0 to 127, as said below
- w_edge_in: bfloat16 [2, 1536, 512], P('segment'), may hold values from -0.15625 to 0.15625
- w_edge_out: bfloat16 [2, 512, 512], P('segment'), may hold values from -0.25 to 0.25
- w_node_in: bfloat16 [2, 1024, 512], P('segment'), may hold values from -0.1875 to 0.1875
- w_node_out: bfloat16 [2, 512, 512], P('segment'), may hold values from -0.25 to 0.25
- gain_edge: float32 [2, 512], P('segment'), may hold values from 0.1 to 1.9
- gain_node: float32 [2, 512], P('segment'), may hold values from 0.1 to 1.9
Outputs:
- node_pair: bfloat16 [2, 4, 8192, 512], P('segment', 'rep', 'dom')
- edge_pair: bfloat16 [2, 4, 24576, 512], P('segment', 'rep', 'dom')
- grad_edge_in: float32 [2, 1536, 512], P('segment', ('dom', 'rep'))
- grad_edge_out: float32 [2, 512, 512], P('segment', ('dom', 'rep'))
- grad_node_in: float32 [2, 1024, 512], P('segment', ('dom', 'rep'))
- grad_node_out: float32 [2, 512, 512], P('segment', ('dom', 'rep'))
- grad_gain_edge: float32 [2, 512], P('segment', ('dom', 'rep'))
- grad_gain_node: float32 [2, 512], P('segment', ('dom', 'rep'))
Inputs may be any that keep to these rules, and one draw needn't show every extreme that they name: `edge_src`: each value is below 192; a value 128 + j * 16 + k of partition p refers to round j only where partition p - o_j exists. `edge_count`: some partition has all 384 slots live. `send_index`: the 16 rows of one partition and round are distinct.
All inputs are finite; a program needn't handle non-finite values.
Results may differ from a plain program's by a relative error of at most 0.039.
Values may be sent and summed in bfloat16 or wider, within the bound.
A program may use at most 128 MiB of HBM per device.

v0:
```python
import functools

import jax
import jax.numpy as jnp
from jax import lax
from jax.experimental import pallas as pl
from jax.experimental.pallas import tpu as pltpu
from jax.sharding import PartitionSpec as P

OFFSETS = (1, -1, 2, -2)
HALO = 16
EPS = 1e-05
MESH = pl.DeviceIdType.MESH
ROWS_A = 48
ROWS_B = 64
GAIN = 16


def reduce_kernel(
    ga, gb, ein_o, eout_o, nin_o, nout_o, gain_o,
    ra1, rb1, a2, ra2, b2, rb2, c3, rc3, fin, rfin, send_sem, recv_sem,
    *, nz, factor,
):
    d = lax.axis_index("dom")
    rep = lax.axis_index("rep")
    z = d // 8
    y = (d // 2) % 4
    xt = (d % 2) * 2 + rep

    def at_y(p):
        return {"dom": z * 8 + p * 2 + d % 2}

    def at_z(p):
        return {"dom": p * 8 + d % 8}

    def at_x(p):
        return {"dom": (d // 2) * 2 + p // 2, "rep": p % 2}

    y_peers = [(y + j) % 4 for j in (1, 2, 3)]
    x_peers = [(xt + j) % 4 for j in (1, 2, 3)]
    z_peers = [(z + j) % nz for j in range(1, nz)]
    barrier = pltpu.get_barrier_semaphore()
    for p in y_peers:
        pl.semaphore_signal(barrier, inc=1, device_id=at_y(p), device_id_type=MESH)
    for p in x_peers:
        pl.semaphore_signal(barrier, inc=1, device_id=at_x(p), device_id_type=MESH)
    for p in z_peers:
        pl.semaphore_signal(barrier, inc=1, device_id=at_z(p), device_id_type=MESH)
    pl.semaphore_wait(barrier, 6 + nz - 1)

    def copy(n, src, dst, device):
        return pltpu.make_async_remote_copy(
            src_ref=src,
            dst_ref=dst,
            send_sem=send_sem.at[n],
            recv_sem=recv_sem.at[n],
            device_id=device,
            device_id_type=MESH,
        )

    first_a = [copy(j, ga.at[p], ra1.at[j], at_y(p)) for j, p in enumerate(y_peers)]
    first_b = [copy(3 + j, gb.at[p], rb1.at[j], at_x(p)) for j, p in enumerate(x_peers)]
    for u, v in zip(first_a, first_b):
        u.start()
        v.start()

    for c in first_a:
        c.wait_recv()
    rows_a = ga.shape[1]

    @pl.loop(0, rows_a // 16)
    def _(i):
        at = pl.ds(pl.multiple_of(i * 16, 16), 16)
        total = ga[y, at, :].astype(jnp.float32)
        for j in range(3):
            total = total + ra1[j, at, :].astype(jnp.float32)
        total = total.astype(jnp.bfloat16)
        for b in range(4):
            a2[b, at, :] = total[:, b * 128 : (b + 1) * 128]

    second_a = [copy(6 + j, a2.at[p], ra2.at[j], at_x(p)) for j, p in enumerate(x_peers)]
    for c in second_a:
        c.start()

    for c in first_b:
        c.wait_recv()

    @pl.loop(0, nz)
    def _(i):
        for q in range(4):
            total = gb[xt, i * 4 + q].astype(jnp.float32)
            for j in range(3):
                total = total + rb1[j, i * 4 + q].astype(jnp.float32)
            b2[q, i] = total.astype(jnp.bfloat16)

    second_b = [copy(9 + j, b2.at[p], rb2.at[j], at_y(p)) for j, p in enumerate(y_peers)]
    for c in second_b:
        c.start()

    for c in second_a:
        c.wait_recv()
    tail = pl.ds(nz * ROWS_A, GAIN)
    gains = a2[xt, tail, :].astype(jnp.float32)
    for j in range(3):
        gains = gains + ra2[j, tail, :].astype(jnp.float32)
    gains = gains.astype(jnp.bfloat16)

    @pl.loop(0, nz)
    def _(i):
        at = pl.ds(pl.multiple_of(i * ROWS_A, 16), ROWS_A)
        total = a2[xt, at, :].astype(jnp.float32)
        for j in range(3):
            total = total + ra2[j, at, :].astype(jnp.float32)
        c3[i, 0:ROWS_A, :] = total.astype(jnp.bfloat16)
        c3[i, ROWS_A : ROWS_A + GAIN, :] = gains

    for c in second_b:
        c.wait_recv()

    @pl.loop(0, nz)
    def _(i):
        total = b2[y, i].astype(jnp.float32)
        for j in range(3):
            total = total + rb2[j, i].astype(jnp.float32)
        c3[i, ROWS_A + GAIN :, :] = total.astype(jnp.bfloat16)

    third = [copy(12 + j, c3.at[p], rc3.at[j], at_z(p)) for j, p in enumerate(z_peers)]
    for c in third:
        c.start()
    total = c3[z].astype(jnp.float32)
    for j, c in enumerate(third):
        c.wait_recv()
        total = total + rc3[j].astype(jnp.float32)
    total = total * factor

    n0 = ROWS_A + GAIN
    for b in range(4):
        fin[b, 0:12, :] = total[12 * b : 12 * b + 12]
        fin[b, 12:16, :] = total[n0 + 32 + 4 * b : n0 + 32 + 4 * b + 4]
        fin[b, 16:24, :] = total[n0 + 8 * b : n0 + 8 * b + 8]
        fin[b, 24:28, :] = total[n0 + 48 + 4 * b : n0 + 48 + 4 * b + 4]
        fin[b, 28:32, :] = total[ROWS_A : ROWS_A + 4]
    base = 12 + nz - 1
    last = [copy(base + j, fin.at[p], rfin.at[xt], at_x(p)) for j, p in enumerate(x_peers)]
    for c in last:
        c.start()
    rfin[xt] = fin[xt]
    for c in last:
        c.wait_recv()
    t = d * 2 + rep
    lane = lax.broadcasted_iota(jnp.int32, (2, 128), 1)
    slot = lax.broadcasted_iota(jnp.int32, (2, 128), 1)
    picked = jnp.zeros((2, 128), jnp.float32)
    for b in range(4):
        cols = slice(b * 128, (b + 1) * 128)
        ein_o[:, cols] = rfin[b, 0:12, :]
        eout_o[:, cols] = rfin[b, 12:16, :]
        nin_o[:, cols] = rfin[b, 16:24, :]
        nout_o[:, cols] = rfin[b, 24:28, :]
        pair = rfin[b, 28:30, :]
        for i in range(4):
            hit = jnp.where(lane + b * 128 == t * 4 + i, pair, 0.0)
            value = jnp.sum(hit, axis=1, keepdims=True)
            picked = picked + jnp.where(slot == i, value, 0.0)
    gain_o[...] = picked
    for c in first_a + first_b + second_a + second_b + third + last:
        c.wait_send()


def reduce_call(ga, gb, factor):
    nz = ga.shape[1] // ROWS_A
    bf, f4 = jnp.bfloat16, jnp.float32
    rows = ga.shape[1]
    vm = pl.BlockSpec(memory_space=pltpu.VMEM)
    copies = 12 + nz - 1 + 3
    return pl.pallas_call(
        functools.partial(reduce_kernel, nz=nz, factor=factor),
        out_shape=[
            jax.ShapeDtypeStruct((12, 512), f4),
            jax.ShapeDtypeStruct((4, 512), f4),
            jax.ShapeDtypeStruct((8, 512), f4),
            jax.ShapeDtypeStruct((4, 512), f4),
            jax.ShapeDtypeStruct((2, 128), f4),
        ],
        in_specs=[vm, vm],
        out_specs=[vm] * 5,
        scratch_shapes=[
            pltpu.VMEM((3, rows, 512), bf),
            pltpu.VMEM((3, 4 * nz, ROWS_B, 128), bf),
            pltpu.VMEM((4, rows, 128), bf),
            pltpu.VMEM((3, rows, 128), bf),
            pltpu.VMEM((4, nz, ROWS_B, 128), bf),
            pltpu.VMEM((3, nz, ROWS_B, 128), bf),
            pltpu.VMEM((nz, 128, 128), bf),
            pltpu.VMEM((nz - 1, 128, 128), bf),
            pltpu.VMEM((4, 32, 128), f4),
            pltpu.VMEM((4, 32, 128), f4),
            pltpu.SemaphoreType.DMA((copies,)),
            pltpu.SemaphoreType.DMA((copies,)),
        ],
        compiler_params=pltpu.CompilerParams(
            collective_id=1, has_side_effects=True, vmem_limit_bytes=40 << 20
        ),
        name="grad_reduce_scatter",
    )(ga, gb)


NODES_DEV = 128
EDGES_DEV = 384
HALOS = 64
TABLE = 192
BLOCK = 32
BF = jnp.bfloat16
F4 = jnp.float32


def mm(a, b):
    return jnp.dot(a, b, preferred_element_type=F4)


def mm_nt(a, b):
    return lax.dot_general(a, b, (((1,), (1,)), ((), ())), preferred_element_type=F4)


def mm_tn(a, b):
    return lax.dot_general(a, b, (((0,), (0,)), ((), ())), preferred_element_type=F4)


def silu_grad(pre):
    sig = jax.nn.sigmoid(pre)
    return sig * (1.0 + pre * (1.0 - sig))


def layer_kernel(
    src_row, dst_row, send_row, count, node_in, edge_in, cot_in,
    w_ein, w_eout, w_nin, w_nout, gain_e, gain_n,
    node_out, edge_out, ga, gb,
    oht, oh, inc, inct, sendt, sendm,
    tab, ein, cn, ce, cn32, halo1, halo2, hs1, hs2, bh,
    sr, pre, mid, tmp, xhat, rstd, enew, agg, pren, midn, tmpn, xhatn, rstdn, hnew,
    doutn, dpren, down, dagg, doute, dpre, gs, gr, de, dh, dge, dgn,
    s_halo1, s_halo2, r_halo, s_fe, r_fe, s_fh, r_fh,
    s_bh, r_bh1, r_bh2, s_be, r_be, s_bo, r_bo,
    l_node, l_edge, l_cot, l_nout, l_eout,
):
    seg = lax.axis_index("segment")
    dom = lax.axis_index("dom")
    n_dom = lax.axis_size("dom")
    first = seg == 0
    second = seg == 1

    def near(step, segment):
        return {"dom": (dom + step + n_dom) % n_dom, "segment": segment}

    barrier = pltpu.get_barrier_semaphore()
    for step in OFFSETS:
        for s in range(2):
            pl.semaphore_signal(barrier, inc=1, device_id=near(step, s), device_id_type=MESH)
    pl.semaphore_signal(barrier, inc=1, device_id={"segment": 1 - seg}, device_id_type=MESH)

    def remote(src, dst, send, recv, device):
        return pltpu.make_async_remote_copy(
            src_ref=src, dst_ref=dst, send_sem=send, recv_sem=recv,
            device_id=device, device_id_type=MESH,
        )

    def load_node(k):
        return pltpu.make_async_copy(node_in.at[k], tab.at[k, 0:NODES_DEV], l_node.at[k])

    def load_edge(k):
        return pltpu.make_async_copy(edge_in.at[k], ein.at[k], l_edge.at[k])

    def load_cot(k):
        return pltpu.make_async_copy(cot_in.at[k], cn.at[k], l_cot.at[k])

    def store_node(src, k):
        return pltpu.make_async_copy(src.at[k], node_out.at[k], l_nout.at[k])

    def store_edge(src, k):
        return pltpu.make_async_copy(src.at[k], edge_out.at[k], l_eout.at[k])

    def halo_copy(src, k, j, sems, segment):
        rows = slice(j * HALO, (j + 1) * HALO)
        into = slice(NODES_DEV + j * HALO, NODES_DEV + (j + 1) * HALO)
        return remote(
            src.at[k, rows], tab.at[k, into], sems.at[k, j], r_halo.at[k, j],
            near(OFFSETS[j], segment),
        )

    def back_copy(dst, k, j, recv):
        rows = slice(j * HALO, (j + 1) * HALO)
        return remote(
            bh.at[k, rows], dst.at[k, rows], s_bh.at[k, j], recv.at[k, j],
            near(-OFFSETS[j], 0),
        )

    def sib_e(k):
        return remote(enew.at[k], ein.at[k], s_fe.at[k], r_fe.at[k], {"segment": 1 - seg})

    def sib_h(k):
        return remote(
            hnew.at[k], tab.at[k, 0:NODES_DEV], s_fh.at[k], r_fh.at[k], {"segment": 1 - seg}
        )

    def sib_de(k):
        return remote(de.at[k], ce.at[k], s_be.at[k], r_be.at[k], {"segment": 1 - seg})

    def sib_do(k):
        return remote(down.at[k], cn32.at[k], s_bo.at[k], r_bo.at[k], {"segment": 1 - seg})

    @pl.when(first)
    def _():
        for k in range(2):
            load_node(k).start()
            load_edge(k).start()

    @pl.when(second)
    def _():
        for k in range(2):
            load_cot(k).start()

    live_count = count[0]
    hot_src = lax.broadcasted_iota(jnp.int32, (TABLE, EDGES_DEV), 0) == src_row[...]
    owner = lax.broadcasted_iota(jnp.int32, (NODES_DEV, EDGES_DEV), 0)
    slot = lax.broadcasted_iota(jnp.int32, (NODES_DEV, EDGES_DEV), 1)
    hot_dst = owner == dst_row[...]
    hot_inc = hot_dst & (slot < live_count)
    f_src = jnp.where(hot_src, 1.0, 0.0)
    f_dst = jnp.where(hot_dst, 1.0, 0.0)
    f_inc = jnp.where(hot_inc, 1.0, 0.0)
    oht[0:TABLE] = f_src.astype(BF)
    oht[TABLE:] = f_dst.astype(BF)
    inc[...] = f_inc.astype(BF)
    oh[:, 0:TABLE] = f_src.T.astype(BF)
    oh[:, TABLE:] = f_dst.T.astype(BF)
    inct[...] = f_inc.T.astype(BF)
    f_send = jnp.where(
        lax.broadcasted_iota(jnp.int32, (NODES_DEV, NODES_DEV), 0) == send_row[...], 1.0, 0.0
    )
    sendt[...] = f_send.astype(BF)
    sendm[...] = f_send.T.astype(BF)
    dge[...] = jnp.zeros_like(dge)
    dgn[...] = jnp.zeros_like(dgn)

    @pl.when(second)
    def _():
        ce[...] = jnp.zeros_like(ce)

    pl.semaphore_wait(barrier, 2 * len(OFFSETS) + 1)

    @pl.when(first)
    def _():
        for k in range(2):
            load_node(k).wait()
            hs1[k] = mm(sendm[0:HALOS], tab[k, 0:NODES_DEV]).astype(BF)
            for j in range(4):
                halo_copy(hs1, k, j, s_halo1, 0).start()

    def mean(v):
        return jnp.sum(v, axis=-1, keepdims=True) * (1.0 / 512.0)

    def norm_block(outer, at, k, x_ref, r_ref):
        center = outer - mean(outer)
        inv = lax.rsqrt(mean(center * center) + EPS)
        hat = center * inv
        x_ref[k, at, :] = hat
        r_ref[k, at, :] = jnp.broadcast_to(inv, (BLOCK, 128))
        return hat

    def norm_back(cot, gain, hat, inv):
        dy = cot * gain
        return inv * (dy - mean(dy) - hat * mean(dy * hat))

    def forward(k):
        @pl.when(first)
        def _():
            load_edge(k).wait()

        @pl.when(second)
        def _():
            sib_e(k).wait_recv()

        pre[k] = mm(ein[k], w_ein[0:512])

        @pl.when(second)
        def _():
            sib_h(k).wait_recv()

        own = tab[k, 0:NODES_DEV]
        sr[TABLE:] = mm(own, w_ein[1024:1536]).astype(BF)
        for j in range(4):
            halo_copy(hs1, k, j, s_halo1, 0).wait_recv()
        sr[0:TABLE] = mm(tab[k], w_ein[512:1024]).astype(BF)
        tmp[...] = mm(oh[...], sr[...])

        @pl.loop(0, EDGES_DEV // BLOCK)
        def _(i):
            at = pl.ds(pl.multiple_of(i * BLOCK, BLOCK), BLOCK)
            v = pre[k, at, :] + tmp[at, :]
            pre[k, at, :] = v
            mid[k, at, :] = (v * jax.nn.sigmoid(v)).astype(BF)

        tmp[...] = mm(mid[k], w_eout[...])

        @pl.loop(0, EDGES_DEV // BLOCK)
        def _(i):
            at = pl.ds(pl.multiple_of(i * BLOCK, BLOCK), BLOCK)
            hat = norm_block(tmp[at, :], at, k, xhat, rstd)
            rows = lax.broadcasted_iota(jnp.int32, (BLOCK, 512), 0) + i * BLOCK
            old = ein[k, at, :].astype(F4)
            enew[k, at, :] = jnp.where(rows < live_count, old + hat * gain_e[...], old).astype(BF)

        @pl.when(first)
        def _():
            sib_e(k).start()

        @pl.when(second)
        def _():
            store_edge(enew, k).start()

        agg[k] = mm(inc[...], enew[k]).astype(BF)
        pren[k] = mm(own, w_nin[0:512]) + mm(agg[k], w_nin[512:1024])

        @pl.loop(0, NODES_DEV // BLOCK)
        def _(i):
            at = pl.ds(pl.multiple_of(i * BLOCK, BLOCK), BLOCK)
            v = pren[k, at, :]
            midn[k, at, :] = (v * jax.nn.sigmoid(v)).astype(BF)

        tmpn[...] = mm(midn[k], w_nout[...])

        @pl.loop(0, NODES_DEV // BLOCK)
        def _(i):
            at = pl.ds(pl.multiple_of(i * BLOCK, BLOCK), BLOCK)
            hat = norm_block(tmpn[at, :], at, k, xhatn, rstdn)
            hnew[k, at, :] = (tab[k, at, :].astype(F4) + hat * gain_n[...]).astype(BF)

        @pl.when(first)
        def _():
            sib_h(k).start()
            hs2[k] = mm(sendm[0:HALOS], hnew[k]).astype(BF)
            for j in range(4):
                halo_copy(hs2, k, j, s_halo2, 1).start()

        @pl.when(second)
        def _():
            store_node(hnew, k).start()

    def backward(k):
        @pl.when(first)
        def _():
            sib_do(k).wait_recv()
            for j in range(4):
                back_copy(halo1, k, j, r_bh1).wait_recv()
            cn[k] = (cn32[k] + mm(sendt[:, 0:HALOS], halo1[k])).astype(BF)

        @pl.when(second)
        def _():
            load_cot(k).wait()

        @pl.loop(0, NODES_DEV // BLOCK)
        def _(i):
            at = pl.ds(pl.multiple_of(i * BLOCK, BLOCK), BLOCK)
            cot = cn[k, at, :].astype(F4)
            hat = xhatn[k, at, :]
            dgn[...] += jnp.sum((cot * hat).reshape(BLOCK // 8, 8, 512), axis=0)
            inv = rstdn[k, at, 0:1]
            doutn[k, at, :] = norm_back(cot, gain_n[...], hat, inv).astype(BF)

        tmpn[...] = mm_nt(doutn[k], w_nout[...])

        @pl.loop(0, NODES_DEV // BLOCK)
        def _(i):
            at = pl.ds(pl.multiple_of(i * BLOCK, BLOCK), BLOCK)
            dpren[k, at, :] = (tmpn[at, :] * silu_grad(pren[k, at, :])).astype(BF)

        dagg[...] = mm_nt(dpren[k], w_nin[512:1024]).astype(BF)

        @pl.when(first)
        def _():
            sib_de(k).wait_recv()

        tmp[...] = mm(inct[...], dagg[...])
        down[k] = cn[k].astype(F4) + mm_nt(dpren[k], w_nin[0:512])

        @pl.loop(0, EDGES_DEV // BLOCK)
        def _(i):
            at = pl.ds(pl.multiple_of(i * BLOCK, BLOCK), BLOCK)
            cot = tmp[at, :] + ce[k, at, :].astype(F4)
            tmp[at, :] = cot
            rows = lax.broadcasted_iota(jnp.int32, (BLOCK, 512), 0) + i * BLOCK
            cot = jnp.where(rows < live_count, cot, 0.0)
            hat = xhat[k, at, :]
            dge[...] += jnp.sum((cot * hat).reshape(BLOCK // 8, 8, 512), axis=0)
            inv = rstd[k, at, 0:1]
            doute[k, at, :] = norm_back(cot, gain_e[...], hat, inv).astype(BF)

        grad = mm_nt(doute[k], w_eout[...])
        pre[k] = grad * silu_grad(pre[k])
        dpre[k] = pre[k].astype(BF)
        gs[k] = mm(oht[0:TABLE], dpre[k]).astype(BF)
        gr[k] = mm(oht[TABLE:], dpre[k]).astype(BF)
        bh[k] = mm_nt(gs[k, NODES_DEV:], w_ein[512:1024]).astype(BF)

        @pl.when(first)
        def _():
            for j in range(4):
                back_copy(halo2, k, j, r_bh2).start()

        @pl.when(second)
        def _():
            for j in range(4):
                back_copy(halo1, k, j, r_bh1).start()

        down[k] += mm_nt(gs[k, 0:NODES_DEV], w_ein[512:1024]) + mm_nt(gr[k], w_ein[1024:1536])

        @pl.when(second)
        def _():
            sib_do(k).start()

        de[k] = (tmp[...] + mm_nt(dpre[k], w_ein[0:512])).astype(BF)

        @pl.when(second)
        def _():
            sib_de(k).start()

        @pl.when(first)
        def _():
            store_edge(de, k).start()

    @pl.loop(0, 4)
    def _(step):
        forward_now = (step == 0) | (step == 1 + seg)
        k = jnp.where(first, step % 2, step // 2)

        @pl.when(forward_now)
        def _():
            forward(k)

        @pl.when(jnp.logical_not(forward_now))
        def _():
            backward(k)

    def put_ein(base, value):
        for q in range(8):
            r = base + q * 16
            row = (r // 192) * ROWS_A + r % ROWS_A
            ga[(r % 192) // ROWS_A, row : row + 16, :] = value[q * 16 : q * 16 + 16].astype(BF)

    def put_b(base, width, offset, value):
        for q in range(128 // width):
            zy = base // width + q
            piece = value[q * width : (q + 1) * width].astype(BF)
            for b in range(4):
                gb[b, zy, offset : offset + width, :] = piece[:, b * 128 : (b + 1) * 128]

    def both(ref):
        return ref[...].reshape(ref.shape[0] * ref.shape[1], ref.shape[2])

    def cols(ref, m):
        return jnp.concatenate([ref[0, :, m * 128 : (m + 1) * 128], ref[1, :, m * 128 : (m + 1) * 128]], axis=0)

    def own_cols(m):
        at = slice(m * 128, (m + 1) * 128)
        return jnp.concatenate([tab[0, 0:NODES_DEV, at], tab[1, 0:NODES_DEV, at]], axis=0)

    for m in range(4):
        base = m * 128
        put_b(base, 16, 48, mm_tn(cols(midn, m), both(doutn)))
        put_b(base, 32, 0, mm_tn(own_cols(m), both(dpren)))
        put_b(512 + base, 32, 0, mm_tn(cols(agg, m), both(dpren)))
        put_b(base, 16, 32, mm_tn(cols(mid, m), both(doute)))
        put_ein(base, mm_tn(cols(ein, m), both(dpre)))
        put_ein(512 + base, mm_tn(cols(tab, m), both(gs)))
        put_ein(1024 + base, mm_tn(own_cols(m), both(gr)))
    row = lax.broadcasted_iota(jnp.int32, (GAIN, 512), 0)
    sum_e = jnp.sum(dge[...], axis=0, keepdims=True)
    sum_n = jnp.sum(dgn[...], axis=0, keepdims=True)
    gains = jnp.where(row == 0, sum_e, jnp.where(row == 1, sum_n, 0.0)).astype(BF)
    for q in range(4):
        ga[q, EDGES_DEV:, :] = gains

    @pl.when(first)
    def _():
        for k in range(2):
            for j in range(4):
                back_copy(halo2, k, j, r_bh2).wait_recv()
            dh[k] = (down[k] + mm(sendt[:, 0:HALOS], halo2[k])).astype(BF)
            store_node(dh, k).start()
        for k in range(2):
            sib_e(k).wait_send()
            sib_h(k).wait_send()
            for j in range(4):
                halo_copy(hs1, k, j, s_halo1, 0).wait_send()
                halo_copy(hs2, k, j, s_halo2, 1).wait_send()
                back_copy(halo2, k, j, r_bh2).wait_send()
            store_edge(de, k).wait()
            store_node(dh, k).wait()

    @pl.when(second)
    def _():
        for k in range(2):
            sib_do(k).wait_send()
            sib_de(k).wait_send()
            for j in range(4):
                back_copy(halo1, k, j, r_bh1).wait_send()
            store_edge(enew, k).wait()
            store_node(hnew, k).wait()


def layer_call(src, dst, send, count, node, edge, cot, weights, gains):
    vm = pl.BlockSpec(memory_space=pltpu.VMEM)
    hbm = pl.BlockSpec(memory_space=pl.ANY)
    smem = pl.BlockSpec(memory_space=pltpu.SMEM)
    nz = 8

    def bf(*shape):
        return pltpu.VMEM(shape, BF)

    def fl(*shape):
        return pltpu.VMEM(shape, F4)

    dma = pltpu.SemaphoreType.DMA
    n, e = NODES_DEV, EDGES_DEV
    return pl.pallas_call(
        layer_kernel,
        out_shape=[
            jax.ShapeDtypeStruct((2, n, 512), BF),
            jax.ShapeDtypeStruct((2, e, 512), BF),
            jax.ShapeDtypeStruct((4, nz * ROWS_A + GAIN, 512), BF),
            jax.ShapeDtypeStruct((4, nz * 4, ROWS_B, 128), BF),
        ],
        in_specs=[vm, vm, vm, smem, hbm, hbm, hbm] + [vm] * 6,
        out_specs=[hbm, hbm, vm, vm],
        scratch_shapes=[
            bf(320, e), bf(e, 320), bf(n, e), bf(e, n), bf(n, n), bf(n, n),
            bf(2, TABLE, 512), bf(2, e, 512), bf(2, n, 512), bf(2, e, 512), fl(2, n, 512),
            bf(2, HALOS, 512), bf(2, HALOS, 512), bf(2, HALOS, 512), bf(2, HALOS, 512), bf(2, HALOS, 512),
            bf(320, 512), fl(2, e, 512), bf(2, e, 512), fl(e, 512), fl(2, e, 512), fl(2, e, 128),
            bf(2, e, 512), bf(2, n, 512), fl(2, n, 512), bf(2, n, 512), fl(n, 512), fl(2, n, 512),
            fl(2, n, 128), bf(2, n, 512),
            bf(2, n, 512), bf(2, n, 512), fl(2, n, 512), bf(n, 512), bf(2, e, 512), bf(2, e, 512),
            bf(2, TABLE, 512), bf(2, n, 512), bf(2, e, 512), bf(2, n, 512), fl(8, 512), fl(8, 512),
            dma((2, 4)), dma((2, 4)), dma((2, 4)), dma((2,)), dma((2,)), dma((2,)), dma((2,)),
            dma((2, 4)), dma((2, 4)), dma((2, 4)), dma((2,)), dma((2,)), dma((2,)), dma((2,)),
            dma((2,)), dma((2,)), dma((2,)), dma((2,)), dma((2,)),
        ],
        compiler_params=pltpu.CompilerParams(
            collective_id=0, has_side_effects=True, vmem_limit_bytes=50 << 20
        ),
        name="layers",
    )(src, dst, send, count, node, edge, cot, *weights, *gains)


def body(
    node_latent, edge_latent, node_cot, edge_src, edge_dst, edge_count, send_index,
    w_edge_in, w_edge_out, w_node_in, w_node_out, gain_edge, gain_node,
):
    micro = node_latent.shape[0]
    factor = float(micro * lax.axis_size("rep") * NODES_DEV * lax.axis_size("dom")) ** (-0.5)
    send = jnp.pad(send_index.reshape(1, HALOS), ((0, 0), (0, NODES_DEV - HALOS)), constant_values=-1)
    node_out, edge_out, ga, gb = layer_call(
        edge_src.reshape(1, EDGES_DEV), edge_dst.reshape(1, EDGES_DEV), send, edge_count,
        node_latent, edge_latent, node_cot,
        (w_edge_in[0], w_edge_out[0], w_node_in[0], w_node_out[0]), (gain_edge, gain_node),
    )
    *shares, picked = reduce_call(ga, gb, factor)
    scaled = [piece[None] for piece in shares]
    return (node_out[None], edge_out[None], *scaled, picked[0:1, :4], picked[1:2, :4])


def solution(mesh):
    placed = (
        P("rep", "dom", None),
        P("rep", "dom", None),
        P("rep", "dom", None),
        P("dom"),
        P("dom"),
        P("dom"),
        P("dom", None, None),
        P("segment", None, None),
        P("segment", None, None),
        P("segment", None, None),
        P("segment", None, None),
        P("segment", None),
        P("segment", None),
    )
    return jax.shard_map(
        body,
        mesh=mesh,
        in_specs=placed,
        out_specs=(
            P("segment", "rep", "dom", None),
            P("segment", "rep", "dom", None),
            P("segment", ("dom", "rep"), None),
            P("segment", ("dom", "rep"), None),
            P("segment", ("dom", "rep"), None),
            P("segment", ("dom", "rep"), None),
            P("segment", ("dom", "rep")),
            P("segment", ("dom", "rep")),
        ),
        check_vma=False,
    )
```

profile of v0, /device:TPU:2, one launch (start us, length us, event | category | flops | bytes accessed | tf_op | source)
XLA Modules:
  0.0 114.4 jit_solution(15271420792999531400)
XLA Ops:
  0.6 0.7 reshape.25.src_row
  1.3 0.7 reshape.26.dst_row
  2.0 0.8 reshape.27
  3.4 0.0 copy-start.2
  3.4 1.1 copy-done.2
  4.6 0.0 copy-start.3
  4.6 1.0 copy-done.3
  5.6 1.0 copy-done.4
  6.6 0.9 copy-done.5
  7.6 0.9 copy-done.6
  8.5 0.7 copy-done.7
  9.2 0.7 copy-done.8
  9.9 60.3 %layers.1 = (bf16[2,128,512]{2,1,0:T(8,128)(2,1)S(1)}, bf16[2,384,512]{2,1,0:T(8,128)(2,1)S(1)}, bf16[4,400,512]{2,1,0:T(8,128)(2,1)}, bf16[4,32,64,128]{3,2,1,0:T(8,128)(2,1)}) custom-call(s32[1,384]{1,0:T(1,128)S(1)} %reshape.25.src_row, s32[1,384]{1,0:T(1,128)S(1)} %reshape.26.dst_row, s32[1,128]{1,0:T(1,128)S(1)} %pad.4.send_row, s32[1]{0:T(128)S(6)} %copy.27.count, ...), custom_call_target="tpu_custom_call" | custom-call | tf_op jit(solution)/shard_map/layers/pallas_call | solution.py:625
  70.2 0.0 copy-start
  70.2 1.6 %copy-done = bf16[4,32,64,128]{3,2,1,0:T(8,128)(2,1)S(1)} copy-done((bf16[4,32,64,128]{3,2,1,0:T(8,128)(2,1)S(1)}, bf16[4,32,64,128]{3,2,1,0:T(8,128)(2,1)}, u32[]{:S(2)}) %copy-start) | copy-done | bytes 2097176
  71.8 1.4 %copy-done.1 = bf16[4,400,512]{2,1,0:T(8,128)(2,1)S(1)} copy-done((bf16[4,400,512]{2,1,0:T(8,128)(2,1)S(1)}, bf16[4,400,512]{2,1,0:T(8,128)(2,1)}, u32[]{:S(2)}) %copy-start.1) | copy-done | bytes 1638424
  73.2 36.6 %grad_reduce_scatter.1 = (f32[12,512]{1,0:T(8,128)S(1)}, f32[4,512]{1,0:T(4,128)S(1)}, f32[8,512]{1,0:T(8,128)S(1)}, f32[4,512]{1,0:T(4,128)S(1)}, f32[2,128]{1,0:T(2,128)S(1)}) custom-call(bf16[4,400,512]{2,1,0:T(8,128)(2,1)S(1)} %copy-done.1, bf16[4,32,64,128]{3,2,1,0:T(8,128)(2,1)S(1)} %copy-done), custom_call_target="tpu_custom_call" | custom-call | tf_op jit(solution)/shard_map/grad_reduce_scatter/pallas_call | solution.py:176
  109.9 0.5 fusion
  110.4 0.6 copy.21
  111.0 0.7 copy.28
  111.7 0.9 copy.29
  112.6 0.6 copy.30
  113.2 0.6 copy.31
  113.8 0.6 copy.32
  (7 shorter events, 0.0 us)
Async XLA Ops:
  3.4 1.1 copy-start.2
  4.6 1.0 copy-start.3
  5.6 1.0 copy-start.4
  6.6 0.9 copy-start.5
  7.6 0.9 copy-start.6
  8.5 0.7 copy-start.7
  9.2 0.7 copy-start.8
  70.2 1.6 %copy-start = (bf16[4,32,64,128]{3,2,1,0:T(8,128)(2,1)S(1)}, bf16[4,32,64,128]{3,2,1,0:T(8,128)(2,1)}, u32[]{:S(2)}) copy-start(bf16[4,32,64,128]{3,2,1,0:T(8,128)(2,1)} %get-tuple-element.20.gb) | copy-start | bytes 6291460
  71.8 1.4 %copy-start.1 = (bf16[4,400,512]{2,1,0:T(8,128)(2,1)S(1)}, bf16[4,400,512]{2,1,0:T(8,128)(2,1)}, u32[]{:S(2)}) copy-start(bf16[4,400,512]{2,1,0:T(8,128)(2,1)} %get-tuple-element.19.ga) | copy-start | bytes 4915204
where the time goes:
time: 115 us; the launch traced here: 114 us
  Pallas kernels  96.9 us (84%)
  local copies, waits for them, and re-layouts  16.2 us (14%)
  between operations  1.33 us (1%)
    pallas_call x1, Pallas kernels, layer_call(): pl.pallas_call(layer_kernel, out_shape=[jax.ShapeDtypeStruct((2, n, 512),...  60.3 us
    pallas_call x1, Pallas kernels, reduce_call(): pl.pallas_call(functools.partial(reduce_kernel, nz=nz, factor=factor), ou...  36.6 us
    unnamed x24, local copies, waits for them, and re-layouts  13.5 us

commit v1 on v0

--- a/solution.py
+++ b/solution.py
@@ -14,197 +14,6 @@
 ROWS_A = 48
 ROWS_B = 64
 GAIN = 16
-
-
-def reduce_kernel(
-    ga, gb, ein_o, eout_o, nin_o, nout_o, gain_o,
-    ra1, rb1, a2, ra2, b2, rb2, c3, rc3, fin, rfin, send_sem, recv_sem,
-    *, nz, factor,
-):
-    d = lax.axis_index("dom")
-    rep = lax.axis_index("rep")
-    z = d // 8
-    y = (d // 2) % 4
-    xt = (d % 2) * 2 + rep
-
-    def at_y(p):
-        return {"dom": z * 8 + p * 2 + d % 2}
-
-    def at_z(p):
-        return {"dom": p * 8 + d % 8}
-
-    def at_x(p):
-        return {"dom": (d // 2) * 2 + p // 2, "rep": p % 2}
-
-    y_peers = [(y + j) % 4 for j in (1, 2, 3)]
-    x_peers = [(xt + j) % 4 for j in (1, 2, 3)]
-    z_peers = [(z + j) % nz for j in range(1, nz)]
-    barrier = pltpu.get_barrier_semaphore()
-    for p in y_peers:
-        pl.semaphore_signal(barrier, inc=1, device_id=at_y(p), device_id_type=MESH)
-    for p in x_peers:
-        pl.semaphore_signal(barrier, inc=1, device_id=at_x(p), device_id_type=MESH)
-    for p in z_peers:
-        pl.semaphore_signal(barrier, inc=1, device_id=at_z(p), device_id_type=MESH)
-    pl.semaphore_wait(barrier, 6 + nz - 1)
-
-    def copy(n, src, dst, device):
-        return pltpu.make_async_remote_copy(
-            src_ref=src,
-            dst_ref=dst,
-            send_sem=send_sem.at[n],
-            recv_sem=recv_sem.at[n],
-            device_id=device,
-            device_id_type=MESH,
-        )
-
-    first_a = [copy(j, ga.at[p], ra1.at[j], at_y(p)) for j, p in enumerate(y_peers)]
-    first_b = [copy(3 + j, gb.at[p], rb1.at[j], at_x(p)) for j, p in enumerate(x_peers)]
-    for u, v in zip(first_a, first_b):
-        u.start()
-        v.start()
-
-    for c in first_a:
-        c.wait_recv()
-    rows_a = ga.shape[1]
-
-    @pl.loop(0, rows_a // 16)
-    def _(i):
-        at = pl.ds(pl.multiple_of(i * 16, 16), 16)
-        total = ga[y, at, :].astype(jnp.float32)
-        for j in range(3):
-            total = total + ra1[j, at, :].astype(jnp.float32)
-        total = total.astype(jnp.bfloat16)
-        for b in range(4):
-            a2[b, at, :] = total[:, b * 128 : (b + 1) * 128]
-
-    second_a = [copy(6 + j, a2.at[p], ra2.at[j], at_x(p)) for j, p in enumerate(x_peers)]
-    for c in second_a:
-        c.start()
-
-    for c in first_b:
-        c.wait_recv()
-
-    @pl.loop(0, nz)
-    def _(i):
-        for q in range(4):
-            total = gb[xt, i * 4 + q].astype(jnp.float32)
-            for j in range(3):
-                total = total + rb1[j, i * 4 + q].astype(jnp.float32)
-            b2[q, i] = total.astype(jnp.bfloat16)
-
-    second_b = [copy(9 + j, b2.at[p], rb2.at[j], at_y(p)) for j, p in enumerate(y_peers)]
-    for c in second_b:
-        c.start()
-
-    for c in second_a:
-        c.wait_recv()
-    tail = pl.ds(nz * ROWS_A, GAIN)
-    gains = a2[xt, tail, :].astype(jnp.float32)
-    for j in range(3):
-        gains = gains + ra2[j, tail, :].astype(jnp.float32)
-    gains = gains.astype(jnp.bfloat16)
-
-    @pl.loop(0, nz)
-    def _(i):
-        at = pl.ds(pl.multiple_of(i * ROWS_A, 16), ROWS_A)
-        total = a2[xt, at, :].astype(jnp.float32)
-        for j in range(3):
-            total = total + ra2[j, at, :].astype(jnp.float32)
-        c3[i, 0:ROWS_A, :] = total.astype(jnp.bfloat16)
-        c3[i, ROWS_A : ROWS_A + GAIN, :] = gains
-
-    for c in second_b:
-        c.wait_recv()
-
-    @pl.loop(0, nz)
-    def _(i):
-        total = b2[y, i].astype(jnp.float32)
-        for j in range(3):
-            total = total + rb2[j, i].astype(jnp.float32)
-        c3[i, ROWS_A + GAIN :, :] = total.astype(jnp.bfloat16)
-
-    third = [copy(12 + j, c3.at[p], rc3.at[j], at_z(p)) for j, p in enumerate(z_peers)]
-    for c in third:
-        c.start()
-    total = c3[z].astype(jnp.float32)
-    for j, c in enumerate(third):
-        c.wait_recv()
-        total = total + rc3[j].astype(jnp.float32)
-    total = total * factor
-
-    n0 = ROWS_A + GAIN
-    for b in range(4):
-        fin[b, 0:12, :] = total[12 * b : 12 * b + 12]
-        fin[b, 12:16, :] = total[n0 + 32 + 4 * b : n0 + 32 + 4 * b + 4]
-        fin[b, 16:24, :] = total[n0 + 8 * b : n0 + 8 * b + 8]
-        fin[b, 24:28, :] = total[n0 + 48 + 4 * b : n0 + 48 + 4 * b + 4]
-        fin[b, 28:32, :] = total[ROWS_A : ROWS_A + 4]
-    base = 12 + nz - 1
-    last = [copy(base + j, fin.at[p], rfin.at[xt], at_x(p)) for j, p in enumerate(x_peers)]
-    for c in last:
-        c.start()
-    rfin[xt] = fin[xt]
-    for c in last:
-        c.wait_recv()
-    t = d * 2 + rep
-    lane = lax.broadcasted_iota(jnp.int32, (2, 128), 1)
-    slot = lax.broadcasted_iota(jnp.int32, (2, 128), 1)
-    picked = jnp.zeros((2, 128), jnp.float32)
-    for b in range(4):
-        cols = slice(b * 128, (b + 1) * 128)
-        ein_o[:, cols] = rfin[b, 0:12, :]
-        eout_o[:, cols] = rfin[b, 12:16, :]
-        nin_o[:, cols] = rfin[b, 16:24, :]
-        nout_o[:, cols] = rfin[b, 24:28, :]
-        pair = rfin[b, 28:30, :]
-        for i in range(4):
-            hit = jnp.where(lane + b * 128 == t * 4 + i, pair, 0.0)
-            value = jnp.sum(hit, axis=1, keepdims=True)
-            picked = picked + jnp.where(slot == i, value, 0.0)
-    gain_o[...] = picked
-    for c in first_a + first_b + second_a + second_b + third + last:
-        c.wait_send()
-
-
-def reduce_call(ga, gb, factor):
-    nz = ga.shape[1] // ROWS_A
-    bf, f4 = jnp.bfloat16, jnp.float32
-    rows = ga.shape[1]
-    vm = pl.BlockSpec(memory_space=pltpu.VMEM)
-    copies = 12 + nz - 1 + 3
-    return pl.pallas_call(
-        functools.partial(reduce_kernel, nz=nz, factor=factor),
-        out_shape=[
-            jax.ShapeDtypeStruct((12, 512), f4),
-            jax.ShapeDtypeStruct((4, 512), f4),
-            jax.ShapeDtypeStruct((8, 512), f4),
-            jax.ShapeDtypeStruct((4, 512), f4),
-            jax.ShapeDtypeStruct((2, 128), f4),
-        ],
-        in_specs=[vm, vm],
-        out_specs=[vm] * 5,
-        scratch_shapes=[
-            pltpu.VMEM((3, rows, 512), bf),
-            pltpu.VMEM((3, 4 * nz, ROWS_B, 128), bf),
-            pltpu.VMEM((4, rows, 128), bf),
-            pltpu.VMEM((3, rows, 128), bf),
-            pltpu.VMEM((4, nz, ROWS_B, 128), bf),
-            pltpu.VMEM((3, nz, ROWS_B, 128), bf),
-            pltpu.VMEM((nz, 128, 128), bf),
-            pltpu.VMEM((nz - 1, 128, 128), bf),
-            pltpu.VMEM((4, 32, 128), f4),
-            pltpu.VMEM((4, 32, 128), f4),
-            pltpu.SemaphoreType.DMA((copies,)),
-            pltpu.SemaphoreType.DMA((copies,)),
-        ],
-        compiler_params=pltpu.CompilerParams(
-            collective_id=1, has_side_effects=True, vmem_limit_bytes=40 << 20
-        ),
-        name="grad_reduce_scatter",
-    )(ga, gb)
-
-
 NODES_DEV = 128
 EDGES_DEV = 384
 HALOS = 64
@@ -232,9 +41,10 @@
 
 
 def layer_kernel(
-    src_row, dst_row, send_row, count, node_in, edge_in, cot_in,
-    w_ein, w_eout, w_nin, w_nout, gain_e, gain_n,
-    node_out, edge_out, ga, gb,
+    src_in, dst_in, send_in, count_in, node_in, edge_in, cot_in,
+    w_ein_in, w_eout_in, w_nin_in, w_nout_in, gain_e_in, gain_n_in,
+    node_out, edge_out, fin_out,
+    src_row, dst_row, send_row, count, w_ein, w_eout, w_nin, w_nout, gain_e, gain_n, l_first,
     oht, oh, inc, inct, sendt, sendm,
     tab, ein, cn, ce, cn32, halo1, halo2, hs1, hs2, bh,
     sr, pre, mid, tmp, xhat, rstd, enew, agg, pren, midn, tmpn, xhatn, rstdn, hnew,
@@ -242,6 +52,9 @@
     s_halo1, s_halo2, r_halo, s_fe, r_fe, s_fh, r_fh,
     s_bh, r_bh1, r_bh2, s_be, r_be, s_bo, r_bo,
     l_node, l_edge, l_cot, l_nout, l_eout,
+    ga, gb, ta, ua, va, tb, ub, vb, a2, ta2, ua2, va2, b2, tb2, ub2, vb2, c3, rc3, fin, rfin,
+    send_sem, recv_sem, l_fin,
+    *, nz, factor,
 ):
     seg = lax.axis_index("segment")
     dom = lax.axis_index("dom")
@@ -252,11 +65,29 @@
     def near(step, segment):
         return {"dom": (dom + step + n_dom) % n_dom, "segment": segment}
 
+    rep = lax.axis_index("rep")
+    z = dom // 8
+    y = (dom // 2) % 4
+    px = rep * 2 + dom % 2
+
+    def at_y(p):
+        return {"dom": z * 8 + p * 2 + dom % 2}
+
+    def at_z(p):
+        return {"dom": p * 8 + dom % 8}
+
+    def at_x(p):
+        return {"dom": (dom // 2) * 2 + p % 2, "rep": p // 2}
+
+    z_peers = [(z + j) % nz for j in range(1, nz)]
+    x_peers = [(px + j) % 4 for j in range(1, 4)]
+    greet = [near(step, s) for step in OFFSETS for s in range(2)]
+    greet += [at_y((y + 1) % 4), at_y((y + 3) % 4)]
+    greet += [at_x(p) for p in x_peers] + [at_z(p) for p in z_peers]
+    greet += [{"segment": 1 - seg}]
     barrier = pltpu.get_barrier_semaphore()
-    for step in OFFSETS:
-        for s in range(2):
-            pl.semaphore_signal(barrier, inc=1, device_id=near(step, s), device_id_type=MESH)
-    pl.semaphore_signal(barrier, inc=1, device_id={"segment": 1 - seg}, device_id_type=MESH)
+    for device in greet:
+        pl.semaphore_signal(barrier, inc=1, device_id=device, device_id_type=MESH)
 
     def remote(src, dst, send, recv, device):
         return pltpu.make_async_remote_copy(
@@ -308,6 +139,24 @@
     def sib_do(k):
         return remote(down.at[k], cn32.at[k], s_bo.at[k], r_bo.at[k], {"segment": 1 - seg})
 
+    small = [
+        pltpu.make_async_copy(u, v, l_first.at[i])
+        for i, (u, v) in enumerate(
+            [
+                (src_in, src_row), (dst_in, dst_row), (send_in, send_row), (count_in, count),
+                (gain_e_in, gain_e), (gain_n_in, gain_n),
+            ]
+        )
+    ]
+    large = [
+        pltpu.make_async_copy(u.at[0], v, l_first.at[6 + i])
+        for i, (u, v) in enumerate(
+            [(w_ein_in, w_ein), (w_eout_in, w_eout), (w_nin_in, w_nin), (w_nout_in, w_nout)]
+        )
+    ]
+    for c in small:
+        c.start()
+
     @pl.when(first)
     def _():
         for k in range(2):
@@ -319,11 +168,15 @@
         for k in range(2):
             load_cot(k).start()
 
+    for c in large:
+        c.start()
+    for c in small:
+        c.wait()
     live_count = count[0]
-    hot_src = lax.broadcasted_iota(jnp.int32, (TABLE, EDGES_DEV), 0) == src_row[...]
+    hot_src = lax.broadcasted_iota(jnp.int32, (TABLE, EDGES_DEV), 0) == src_row[...].reshape(1, EDGES_DEV)
     owner = lax.broadcasted_iota(jnp.int32, (NODES_DEV, EDGES_DEV), 0)
     slot = lax.broadcasted_iota(jnp.int32, (NODES_DEV, EDGES_DEV), 1)
-    hot_dst = owner == dst_row[...]
+    hot_dst = owner == dst_row[...].reshape(1, EDGES_DEV)
     hot_inc = hot_dst & (slot < live_count)
     f_src = jnp.where(hot_src, 1.0, 0.0)
     f_dst = jnp.where(hot_dst, 1.0, 0.0)
@@ -334,9 +187,9 @@
     oh[:, 0:TABLE] = f_src.T.astype(BF)
     oh[:, TABLE:] = f_dst.T.astype(BF)
     inct[...] = f_inc.T.astype(BF)
-    f_send = jnp.where(
-        lax.broadcasted_iota(jnp.int32, (NODES_DEV, NODES_DEV), 0) == send_row[...], 1.0, 0.0
-    )
+    node = lax.broadcasted_iota(jnp.int32, (NODES_DEV, HALO), 0)
+    hots = [jnp.where(node == send_row[0, j : j + 1, :], 1.0, 0.0) for j in range(4)]
+    f_send = jnp.concatenate(hots + [jnp.zeros((NODES_DEV, NODES_DEV - HALOS), F4)], axis=1)
     sendt[...] = f_send.astype(BF)
     sendm[...] = f_send.T.astype(BF)
     dge[...] = jnp.zeros_like(dge)
@@ -346,7 +199,10 @@
     def _():
         ce[...] = jnp.zeros_like(ce)
 
-    pl.semaphore_wait(barrier, 2 * len(OFFSETS) + 1)
+    pl.semaphore_wait(barrier, len(greet))
+
+    for c in large:
+        c.wait()
 
     @pl.when(first)
     def _():
@@ -564,12 +420,62 @@
         at = slice(m * 128, (m + 1) * 128)
         return jnp.concatenate([tab[0, 0:NODES_DEV, at], tab[1, 0:NODES_DEV, at]], axis=0)
 
+    def copy(n, src, dst, device):
+        return remote(src, dst, send_sem.at[n], recv_sem.at[n], device)
+
+    class Ring:
+        def __init__(self, base, src, t, u, v, me, at, cut):
+            right, left, across = (me + 1) % 4, (me + 3) % 4, (me + 2) % 4
+            lo, hi = slice(0, cut), slice(cut, t.shape[0])
+            self.out = [
+                copy(base, src.at[across, lo], t.at[lo], at(right)),
+                copy(base + 1, src.at[across, hi], t.at[hi], at(left)),
+                copy(base + 2, src.at[right, hi], u.at[hi], at(right)),
+                copy(base + 3, src.at[left, lo], v.at[lo], at(left)),
+                copy(base + 4, t.at[lo], u.at[lo], at(right)),
+                copy(base + 5, t.at[hi], v.at[hi], at(left)),
+            ]
+            self.src, self.t, self.u, self.v = src, t, u, v
+            self.me, self.right, self.left, self.cut = me, right, left, cut
+
+        def start(self):
+            for c in self.out[:4]:
+                c.start()
+
+        def middle(self, block):
+            src, t, n, cut = self.src, self.t, self.t.shape[0], self.cut
+            for c, q, lo, hi in ((0, self.right, 0, cut), (1, self.left, cut, n)):
+                self.out[c].wait_recv()
+
+                @pl.loop(lo // block, hi // block)
+                def _(i):
+                    at = pl.ds(pl.multiple_of(i * block, block), block)
+                    t[at] = (t[at].astype(F4) + src[q, at].astype(F4)).astype(BF)
+
+                self.out[4 + c].start()
+
+        def total(self, at):
+            own = self.src[self.me, at].astype(F4)
+            return own + self.u[at].astype(F4) + self.v[at].astype(F4)
+
+        def arrive(self):
+            for c in self.out[2:]:
+                c.wait_recv()
+
+    ring_a = Ring(0, ga, ta, ua, va, y, at_y, 208)
+    ring_b = Ring(6, gb, tb, ub, vb, px, at_x, 2 * nz)
+    ring_a2 = Ring(12, a2, ta2, ua2, va2, px, at_x, 208)
+    ring_b2 = Ring(18, b2, tb2, ub2, vb2, y, at_y, nz // 2)
+
     for m in range(4):
         base = m * 128
         put_b(base, 16, 48, mm_tn(cols(midn, m), both(doutn)))
         put_b(base, 32, 0, mm_tn(own_cols(m), both(dpren)))
         put_b(512 + base, 32, 0, mm_tn(cols(agg, m), both(dpren)))
         put_b(base, 16, 32, mm_tn(cols(mid, m), both(doute)))
+    ring_b.start()
+    for m in range(4):
+        base = m * 128
         put_ein(base, mm_tn(cols(ein, m), both(dpre)))
         put_ein(512 + base, mm_tn(cols(tab, m), both(gs)))
         put_ein(1024 + base, mm_tn(own_cols(m), both(gr)))
@@ -579,6 +485,7 @@
     gains = jnp.where(row == 0, sum_e, jnp.where(row == 1, sum_n, 0.0)).astype(BF)
     for q in range(4):
         ga[q, EDGES_DEV:, :] = gains
+    ring_a.start()
 
     @pl.when(first)
     def _():
@@ -587,6 +494,76 @@
                 back_copy(halo2, k, j, r_bh2).wait_recv()
             dh[k] = (down[k] + mm(sendt[:, 0:HALOS], halo2[k])).astype(BF)
             store_node(dh, k).start()
+
+    ring_a.middle(16)
+    ring_b.middle(1)
+    ring_a.arrive()
+
+    @pl.loop(0, ga.shape[1] // 16)
+    def _(i):
+        at = pl.ds(pl.multiple_of(i * 16, 16), 16)
+        total = ring_a.total(at).astype(BF)
+        for b in range(4):
+            a2[b, at, :] = total[:, b * 128 : (b + 1) * 128]
+
+    ring_a2.start()
+    ring_b.arrive()
+
+    @pl.loop(0, nz)
+    def _(i):
+        for q in range(4):
+            b2[q, i] = ring_b.total(i * 4 + q).astype(BF)
+
+    ring_b2.start()
+    ring_a2.middle(16)
+    ring_b2.middle(1)
+    ring_a2.arrive()
+    gains = ring_a2.total(slice(nz * ROWS_A, nz * ROWS_A + GAIN)).astype(BF)
+
+    @pl.loop(0, nz)
+    def _(i):
+        at = pl.ds(pl.multiple_of(i * ROWS_A, 16), ROWS_A)
+        c3[i, 0:ROWS_A, :] = ring_a2.total(at).astype(BF)
+        c3[i, ROWS_A : ROWS_A + GAIN, :] = gains
+
+    ring_b2.arrive()
+
+    @pl.loop(0, nz)
+    def _(i):
+        c3[i, ROWS_A + GAIN :, :] = ring_b2.total(i).astype(BF)
+
+    third = [copy(24 + j, c3.at[p], rc3.at[j], at_z(p)) for j, p in enumerate(z_peers)]
+    for c in third:
+        c.start()
+    total = c3[z].astype(F4)
+    for j, c in enumerate(third):
+        c.wait_recv()
+        total = total + rc3[j].astype(F4)
+    total = total * factor
+
+    n0 = ROWS_A + GAIN
+    for p in range(4):
+        b = (p % 2) * 2 + p // 2
+        fin[p, 0:12, :] = total[12 * b : 12 * b + 12]
+        fin[p, 12:16, :] = total[n0 + 32 + 4 * b : n0 + 32 + 4 * b + 4]
+        fin[p, 16:24, :] = total[n0 + 8 * b : n0 + 8 * b + 8]
+        fin[p, 24:28, :] = total[n0 + 48 + 4 * b : n0 + 48 + 4 * b + 4]
+        fin[p, 28:32, :] = total[ROWS_A : ROWS_A + 4]
+    base = 24 + nz - 1
+    last = [copy(base + j, fin.at[p], rfin.at[px], at_x(p)) for j, p in enumerate(x_peers)]
+    for c in last:
+        c.start()
+    rfin[px] = fin[px]
+    for c in last:
+        c.wait_recv()
+    result = pltpu.make_async_copy(rfin, fin_out, l_fin.at[0])
+    result.start()
+    result.wait()
+    for c in ring_a.out + ring_b.out + ring_a2.out + ring_b2.out + third + last:
+        c.wait_send()
+
+    @pl.when(first)
+    def _():
         for k in range(2):
             sib_e(k).wait_send()
             sib_h(k).wait_send()
@@ -608,11 +585,10 @@
             store_node(hnew, k).wait()
 
 
-def layer_call(src, dst, send, count, node, edge, cot, weights, gains):
-    vm = pl.BlockSpec(memory_space=pltpu.VMEM)
+def layer_call(operands, factor):
     hbm = pl.BlockSpec(memory_space=pl.ANY)
-    smem = pl.BlockSpec(memory_space=pltpu.SMEM)
     nz = 8
+    i32 = jnp.int32
 
     def bf(*shape):
         return pltpu.VMEM(shape, BF)
@@ -622,17 +598,20 @@
 
     dma = pltpu.SemaphoreType.DMA
     n, e = NODES_DEV, EDGES_DEV
+    rows = nz * ROWS_A + GAIN
+    copies = 24 + nz - 1 + 3
     return pl.pallas_call(
-        layer_kernel,
+        functools.partial(layer_kernel, nz=nz, factor=factor),
         out_shape=[
             jax.ShapeDtypeStruct((2, n, 512), BF),
             jax.ShapeDtypeStruct((2, e, 512), BF),
-            jax.ShapeDtypeStruct((4, nz * ROWS_A + GAIN, 512), BF),
-            jax.ShapeDtypeStruct((4, nz * 4, ROWS_B, 128), BF),
+            jax.ShapeDtypeStruct((4, 32, 128), F4),
         ],
-        in_specs=[vm, vm, vm, smem, hbm, hbm, hbm] + [vm] * 6,
-        out_specs=[hbm, hbm, vm, vm],
+        in_specs=[hbm] * 13,
+        out_specs=[hbm] * 3,
         scratch_shapes=[
+            pltpu.VMEM((e,), i32), pltpu.VMEM((e,), i32), pltpu.VMEM((1, 4, HALO), i32), pltpu.SMEM((1,), i32),
+            bf(1536, 512), bf(512, 512), bf(1024, 512), bf(512, 512), fl(1, 512), fl(1, 512), dma((10,)),
             bf(320, e), bf(e, 320), bf(n, e), bf(e, n), bf(n, n), bf(n, n),
             bf(2, TABLE, 512), bf(2, e, 512), bf(2, n, 512), bf(2, e, 512), fl(2, n, 512),
             bf(2, HALOS, 512), bf(2, HALOS, 512), bf(2, HALOS, 512), bf(2, HALOS, 512), bf(2, HALOS, 512),
@@ -644,12 +623,74 @@
             dma((2, 4)), dma((2, 4)), dma((2, 4)), dma((2,)), dma((2,)), dma((2,)), dma((2,)),
             dma((2, 4)), dma((2, 4)), dma((2, 4)), dma((2,)), dma((2,)), dma((2,)), dma((2,)),
             dma((2,)), dma((2,)), dma((2,)), dma((2,)), dma((2,)),
+            bf(4, rows, 512), bf(4, 4 * nz, ROWS_B, 128),
+            bf(rows, 512), bf(rows, 512), bf(rows, 512),
+            bf(4 * nz, ROWS_B, 128), bf(4 * nz, ROWS_B, 128), bf(4 * nz, ROWS_B, 128),
+            bf(4, rows, 128), bf(rows, 128), bf(rows, 128), bf(rows, 128),
+            bf(4, nz, ROWS_B, 128), bf(nz, ROWS_B, 128), bf(nz, ROWS_B, 128), bf(nz, ROWS_B, 128),
+            bf(nz, 128, 128), bf(nz - 1, 128, 128), fl(4, 32, 128), fl(4, 32, 128),
+            dma((copies,)), dma((copies,)), dma((1,)),
         ],
         compiler_params=pltpu.CompilerParams(
-            collective_id=0, has_side_effects=True, vmem_limit_bytes=50 << 20
+            collective_id=0, has_side_effects=True, vmem_limit_bytes=56 << 20
         ),
         name="layers",
-    )(src, dst, send, count, node, edge, cot, *weights, *gains)
+    )(*operands)
+
+
+def finish_kernel(
+    node_in, edge_in, fin_in, node_o, edge_o, ein_o, eout_o, nin_o, nout_o, ge_o, gn_o, rfin, sems
+):
+    first = pltpu.make_async_copy(fin_in, rfin, sems.at[0])
+    first.start()
+    moves = [pltpu.make_async_copy(node_in, node_o.at[0], sems.at[1])]
+    moves += [
+        pltpu.make_async_copy(edge_in.at[k], edge_o.at[0, k], sems.at[2 + k]) for k in range(2)
+    ]
+    for c in moves:
+        c.start()
+    first.wait()
+    t = lax.axis_index("dom") * 2 + lax.axis_index("rep")
+    lane = lax.broadcasted_iota(jnp.int32, (2, 128), 1)
+    picked = jnp.zeros((2, 128), F4)
+    for b in range(4):
+        at = slice(b * 128, (b + 1) * 128)
+        ein_o[0, :, at] = rfin[b, 0:12, :]
+        eout_o[0, :, at] = rfin[b, 12:16, :]
+        nin_o[0, :, at] = rfin[b, 16:24, :]
+        nout_o[0, :, at] = rfin[b, 24:28, :]
+        pair = rfin[b, 28:30, :]
+        for i in range(4):
+            hit = jnp.where(lane + b * 128 == t * 4 + i, pair, 0.0)
+            value = jnp.sum(hit, axis=1, keepdims=True)
+            picked = picked + jnp.where(lane == i, value, 0.0)
+    ge_o[...] = picked[0:1, 0:4]
+    gn_o[...] = picked[1:2, 0:4]
+    for c in moves:
+        c.wait()
+
+
+def finish_call(node, edge, fin):
+    hbm = pl.BlockSpec(memory_space=pl.ANY)
+    vm = pl.BlockSpec(memory_space=pltpu.VMEM)
+    return pl.pallas_call(
+        finish_kernel,
+        out_shape=[
+            jax.ShapeDtypeStruct((1, *node.shape), BF),
+            jax.ShapeDtypeStruct((1, *edge.shape), BF),
+            jax.ShapeDtypeStruct((1, 12, 512), F4),
+            jax.ShapeDtypeStruct((1, 4, 512), F4),
+            jax.ShapeDtypeStruct((1, 8, 512), F4),
+            jax.ShapeDtypeStruct((1, 4, 512), F4),
+            jax.ShapeDtypeStruct((1, 4), F4),
+            jax.ShapeDtypeStruct((1, 4), F4),
+        ],
+        in_specs=[hbm] * 3,
+        out_specs=[hbm] * 2 + [vm] * 6,
+        scratch_shapes=[pltpu.VMEM((4, 32, 128), F4), pltpu.SemaphoreType.DMA((4,))],
+        compiler_params=pltpu.CompilerParams(vmem_limit_bytes=56 << 20),
+        name="finish",
+    )(node, edge, fin)
 
 
 def body(
@@ -658,15 +699,14 @@
 ):
     micro = node_latent.shape[0]
     factor = float(micro * lax.axis_size("rep") * NODES_DEV * lax.axis_size("dom")) ** (-0.5)
-    send = jnp.pad(send_index.reshape(1, HALOS), ((0, 0), (0, NODES_DEV - HALOS)), constant_values=-1)
-    node_out, edge_out, ga, gb = layer_call(
-        edge_src.reshape(1, EDGES_DEV), edge_dst.reshape(1, EDGES_DEV), send, edge_count,
-        node_latent, edge_latent, node_cot,
-        (w_edge_in[0], w_edge_out[0], w_node_in[0], w_node_out[0]), (gain_edge, gain_node),
+    node, edge, fin = layer_call(
+        (
+            edge_src, edge_dst, send_index, edge_count, node_latent, edge_latent, node_cot,
+            w_edge_in, w_edge_out, w_node_in, w_node_out, gain_edge, gain_node,
+        ),
+        factor,
     )
-    *shares, picked = reduce_call(ga, gb, factor)
-    scaled = [piece[None] for piece in shares]
-    return (node_out[None], edge_out[None], *scaled, picked[0:1, :4], picked[1:2, :4])
+    return tuple(finish_call(node, edge, fin))
 
 
 def solution(mesh):

time: 115 us -> 124 us (1.078)
  Pallas kernels: 96.9 us -> 120 us
  local copies, waits for them, and re-layouts: 16.2 us -> 1.39 us
    pallas_call x2, Pallas kernels: 96.9 us -> 120 us  [the longest x1 86.3 us: layer_call(): pl.pallas_call(functools.partial(layer_kernel, nz=nz, factor=factor), out...]
    unnamed x24 -> x0, local copies, waits for them, and re-layouts: 13.5 us -> none
    reshape x3 -> x0, local copies, waits for them, and re-layouts: 2.13 us -> none  [the longest x1 0.76 us: body(): send_index.reshape(1, HALOS)]
    pallas_call x0 -> x1, local copies, waits for them, and re-layouts: none -> 1.39 us  [finish_call(): pl.pallas_call(finish_kernel, out_shape=[jax.ShapeDtypeStruct((1, *node.s...]
where the time goes in v1:
time: 124 us; the launch traced here: 122 us
  Pallas kernels  120 us (97%)
  local copies, waits for them, and re-layouts  1.39 us (1%)
  between operations  1.3 us (1%)
    pallas_call x1, Pallas kernels, layer_call(): pl.pallas_call(functools.partial(layer_kernel, nz=nz, factor=factor), out...  86.3 us
    pallas_call x1, Pallas kernels, finish_call(): pl.pallas_call(finish_kernel, out_shape=[jax.ShapeDtypeStruct((1, *node.s...  33.5 us

profile of v1, /device:TPU:2, one launch (start us, length us, event | category | flops | bytes accessed | tf_op | source)
XLA Modules:
  0.0 122.5 jit_solution(15592040408872973665)
XLA Ops:
  1.3 86.3 %layers.1 = (bf16[2,128,512]{2,1,0:T(8,128)(2,1)}, bf16[2,384,512]{2,1,0:T(8,128)(2,1)}, f32[4,32,128]{2,1,0:T(8,128)}) custom-call(s32[384]{0:T(512)} %src_in.1, s32[384]{0:T(512)} %dst_in.1, s32[1,4,16]{2,1,0:T(4,128)} %send_in.1, s32[1]{0:T(128)S(6)} %copy.22.count_in, bf16[2,128,512]{2,1,0:T(8,128)(2,1)} %node_in.1, bf16[2,384,512]{2,1,0:T(8,128)(2,1)} %edge_in.1, ...), custom_call_target="tpu_custom_call" | custom-call | tf_op jit(solution)/shard_map/layers/pallas_call | solution.py:603
  87.6 33.5 %finish.1 = (bf16[1,2,128,512]{3,2,1,0:T(8,128)(2,1)}, bf16[1,2,384,512]{3,2,1,0:T(8,128)(2,1)}, f32[1,12,512]{2,1,0:T(8,128)}, f32[1,4,512]{2,1,0:T(4,128)}, f3...) custom-call(bf16[2,128,512]{2,1,0:T(8,128)(2,1)} %get-tuple-element.11.node_in, ...), custom_call_target="tpu_custom_call" | custom-call | tf_op jit(solution)/shard_map/finish/pallas_call | solution.py:676
  121.1 1.4 %copy.21 = f32[1,12,512]{2,0,1:T(1,128)} copy(f32[1,12,512]{2,1,0:T(8,128)} %get-tuple-element.16) | data formatting | bytes 49152 | tf_op jit(solution)/shard_map/finish/pallas_call | solution.py:676

commit v2 on v1

--- a/solution.py
+++ b/solution.py
@@ -639,23 +639,31 @@
 
 
 def finish_kernel(
-    node_in, edge_in, fin_in, node_o, edge_o, ein_o, eout_o, nin_o, nout_o, ge_o, gn_o, rfin, sems
+    node_in, edge_in, fin_in, node_o, edge_o, ein_o, eout_o, nin_o, nout_o, ge_o, gn_o,
+    rfin, node_v, edge_v, sems, out_sems,
 ):
     first = pltpu.make_async_copy(fin_in, rfin, sems.at[0])
     first.start()
-    moves = [pltpu.make_async_copy(node_in, node_o.at[0], sems.at[1])]
-    moves += [
-        pltpu.make_async_copy(edge_in.at[k], edge_o.at[0, k], sems.at[2 + k]) for k in range(2)
-    ]
+    parts = [(node_in.at[k], node_v.at[k], node_o.at[0, k]) for k in range(2)]
+    for k in range(2):
+        for q in range(2):
+            at = slice(q * 192, q * 192 + 192)
+            parts.append((edge_in.at[k, at], edge_v.at[k, at], edge_o.at[0, k, at]))
+    moves = [pltpu.make_async_copy(u, v, sems.at[1 + i]) for i, (u, v, _) in enumerate(parts)]
+    stores = [pltpu.make_async_copy(v, w, out_sems.at[i]) for i, (_, v, w) in enumerate(parts)]
     for c in moves:
         c.start()
+    for c, w in zip(moves, stores):
+        c.wait()
+        w.start()
     first.wait()
     t = lax.axis_index("dom") * 2 + lax.axis_index("rep")
     lane = lax.broadcasted_iota(jnp.int32, (2, 128), 1)
     picked = jnp.zeros((2, 128), F4)
     for b in range(4):
         at = slice(b * 128, (b + 1) * 128)
-        ein_o[0, :, at] = rfin[b, 0:12, :]
+        for r in range(12):
+            ein_o[r, :, at] = rfin[b, r : r + 1, :]
         eout_o[0, :, at] = rfin[b, 12:16, :]
         nin_o[0, :, at] = rfin[b, 16:24, :]
         nout_o[0, :, at] = rfin[b, 24:28, :]
@@ -666,7 +674,7 @@
             picked = picked + jnp.where(lane == i, value, 0.0)
     ge_o[...] = picked[0:1, 0:4]
     gn_o[...] = picked[1:2, 0:4]
-    for c in moves:
+    for c in stores:
         c.wait()
 
 
@@ -678,7 +686,7 @@
         out_shape=[
             jax.ShapeDtypeStruct((1, *node.shape), BF),
             jax.ShapeDtypeStruct((1, *edge.shape), BF),
-            jax.ShapeDtypeStruct((1, 12, 512), F4),
+            jax.ShapeDtypeStruct((12, 1, 512), F4),
             jax.ShapeDtypeStruct((1, 4, 512), F4),
             jax.ShapeDtypeStruct((1, 8, 512), F4),
             jax.ShapeDtypeStruct((1, 4, 512), F4),
@@ -687,7 +695,10 @@
         ],
         in_specs=[hbm] * 3,
         out_specs=[hbm] * 2 + [vm] * 6,
-        scratch_shapes=[pltpu.VMEM((4, 32, 128), F4), pltpu.SemaphoreType.DMA((4,))],
+        scratch_shapes=[
+            pltpu.VMEM((4, 32, 128), F4), pltpu.VMEM(node.shape, BF), pltpu.VMEM(edge.shape, BF),
+            pltpu.SemaphoreType.DMA((7,)), pltpu.SemaphoreType.DMA((6,)),
+        ],
         compiler_params=pltpu.CompilerParams(vmem_limit_bytes=56 << 20),
         name="finish",
     )(node, edge, fin)
@@ -706,7 +717,8 @@
         ),
         factor,
     )
-    return tuple(finish_call(node, edge, fin))
+    node, edge, ein, *rest = finish_call(node, edge, fin)
+    return (node, edge, jnp.swapaxes(ein, 0, 1), *rest)
 
 
 def solution(mesh):

time: 124 us -> 91.3 us (0.74)
  Pallas kernels: 120 us -> 89 us
  local copies, waits for them, and re-layouts: 1.39 us -> 0 us
    pallas_call x1, Pallas kernels: 33.5 us -> 2.73 us  [finish_call(): pl.pallas_call(finish_kernel, out_shape=[jax.ShapeDtypeStruct((1, *node.s...]
    pallas_call x1 -> x0, local copies, waits for them, and re-layouts: 1.39 us -> none  [finish_call(): pl.pallas_call(finish_kernel, out_shape=[jax.ShapeDtypeStruct((1, *node.s...]
where the time goes in v2:
time: 91.3 us; the launch traced here: 90.3 us
  Pallas kernels  89 us (97%)
  between operations  1.29 us (1%)
    pallas_call x1, Pallas kernels, layer_call(): pl.pallas_call(functools.partial(layer_kernel, nz=nz, factor=factor), out...  86.3 us
    pallas_call x1, Pallas kernels, finish_call(): pl.pallas_call(finish_kernel, out_shape=[jax.ShapeDtypeStruct((1, *node.s...  2.73 us

profile of v2, /device:TPU:2, one launch (start us, length us, event | category | flops | bytes accessed | tf_op | source)
XLA Modules:
  0.0 90.3 jit_solution(4777767995223397480)
XLA Ops:
  1.3 86.3 %layers.1 = (bf16[2,128,512]{2,1,0:T(8,128)(2,1)}, bf16[2,384,512]{2,1,0:T(8,128)(2,1)}, f32[4,32,128]{2,1,0:T(8,128)}) custom-call(s32[384]{0:T(512)} %src_in.1, s32[384]{0:T(512)} %dst_in.1, s32[1,4,16]{2,1,0:T(4,128)} %send_in.1, s32[1]{0:T(128)S(6)} %copy.21.count_in, bf16[2,128,512]{2,1,0:T(8,128)(2,1)} %node_in.1, bf16[2,384,512]{2,1,0:T(8,128)(2,1)} %edge_in.1, ...), custom_call_target="tpu_custom_call" | custom-call | tf_op jit(solution)/shard_map/layers/pallas_call | solution.py:603
  87.6 2.7 %finish.1 = (bf16[1,2,128,512]{3,2,1,0:T(8,128)(2,1)}, bf16[1,2,384,512]{3,2,1,0:T(8,128)(2,1)}, f32[12,1,512]{2,1,0:T(1,128)}, f32[1,4,512]{2,1,0:T(4,128)}, f3...) custom-call(bf16[2,128,512]{2,1,0:T(8,128)(2,1)} %get-tuple-element.19.node_in, ...), custom_call_target="tpu_custom_call" | custom-call | tf_op jit(solution)/shard_map/finish/pallas_call | solution.py:684

commit v3 on v2

--- a/solution.py
+++ b/solution.py
@@ -18,7 +18,7 @@
 EDGES_DEV = 384
 HALOS = 64
 TABLE = 192
-BLOCK = 32
+BLOCK = 128
 BF = jnp.bfloat16
 F4 = jnp.float32
 
@@ -172,6 +172,26 @@
         c.start()
     for c in small:
         c.wait()
+    node = lax.broadcasted_iota(jnp.int32, (NODES_DEV, HALO), 0)
+    hots = [jnp.where(node == send_row[0, j : j + 1, :], 1.0, 0.0) for j in range(4)]
+    f_send = jnp.concatenate(hots + [jnp.zeros((NODES_DEV, NODES_DEV - HALOS), F4)], axis=1)
+    sendt[...] = f_send.astype(BF)
+    sendm[...] = f_send.T.astype(BF)
+
+    @pl.when(first)
+    def _():
+        for k in range(2):
+            load_node(k).wait()
+            hs1[k] = mm(sendm[0:HALOS], tab[k, 0:NODES_DEV]).astype(BF)
+
+    pl.semaphore_wait(barrier, len(greet))
+
+    @pl.when(first)
+    def _():
+        for k in range(2):
+            for j in range(4):
+                halo_copy(hs1, k, j, s_halo1, 0).start()
+
     live_count = count[0]
     hot_src = lax.broadcasted_iota(jnp.int32, (TABLE, EDGES_DEV), 0) == src_row[...].reshape(1, EDGES_DEV)
     owner = lax.broadcasted_iota(jnp.int32, (NODES_DEV, EDGES_DEV), 0)
@@ -187,11 +207,6 @@
     oh[:, 0:TABLE] = f_src.T.astype(BF)
     oh[:, TABLE:] = f_dst.T.astype(BF)
     inct[...] = f_inc.T.astype(BF)
-    node = lax.broadcasted_iota(jnp.int32, (NODES_DEV, HALO), 0)
-    hots = [jnp.where(node == send_row[0, j : j + 1, :], 1.0, 0.0) for j in range(4)]
-    f_send = jnp.concatenate(hots + [jnp.zeros((NODES_DEV, NODES_DEV - HALOS), F4)], axis=1)
-    sendt[...] = f_send.astype(BF)
-    sendm[...] = f_send.T.astype(BF)
     dge[...] = jnp.zeros_like(dge)
     dgn[...] = jnp.zeros_like(dgn)
 
@@ -199,18 +214,8 @@
     def _():
         ce[...] = jnp.zeros_like(ce)
 
-    pl.semaphore_wait(barrier, len(greet))
-
     for c in large:
         c.wait()
-
-    @pl.when(first)
-    def _():
-        for k in range(2):
-            load_node(k).wait()
-            hs1[k] = mm(sendm[0:HALOS], tab[k, 0:NODES_DEV]).astype(BF)
-            for j in range(4):
-                halo_copy(hs1, k, j, s_halo1, 0).start()
 
     def mean(v):
         return jnp.sum(v, axis=-1, keepdims=True) * (1.0 / 512.0)
@@ -249,7 +254,7 @@
         sr[0:TABLE] = mm(tab[k], w_ein[512:1024]).astype(BF)
         tmp[...] = mm(oh[...], sr[...])
 
-        @pl.loop(0, EDGES_DEV // BLOCK)
+        @pl.loop(0, EDGES_DEV // BLOCK, unroll=True)
         def _(i):
             at = pl.ds(pl.multiple_of(i * BLOCK, BLOCK), BLOCK)
             v = pre[k, at, :] + tmp[at, :]
@@ -258,7 +263,7 @@
 
         tmp[...] = mm(mid[k], w_eout[...])
 
-        @pl.loop(0, EDGES_DEV // BLOCK)
+        @pl.loop(0, EDGES_DEV // BLOCK, unroll=True)
         def _(i):
             at = pl.ds(pl.multiple_of(i * BLOCK, BLOCK), BLOCK)
             hat = norm_block(tmp[at, :], at, k, xhat, rstd)
@@ -277,7 +282,7 @@
         agg[k] = mm(inc[...], enew[k]).astype(BF)
         pren[k] = mm(own, w_nin[0:512]) + mm(agg[k], w_nin[512:1024])
 
-        @pl.loop(0, NODES_DEV // BLOCK)
+        @pl.loop(0, NODES_DEV // BLOCK, unroll=True)
         def _(i):
             at = pl.ds(pl.multiple_of(i * BLOCK, BLOCK), BLOCK)
             v = pren[k, at, :]
@@ -285,7 +290,7 @@
 
         tmpn[...] = mm(midn[k], w_nout[...])
 
-        @pl.loop(0, NODES_DEV // BLOCK)
+        @pl.loop(0, NODES_DEV // BLOCK, unroll=True)
         def _(i):
             at = pl.ds(pl.multiple_of(i * BLOCK, BLOCK), BLOCK)
             hat = norm_block(tmpn[at, :], at, k, xhatn, rstdn)
@@ -314,7 +319,7 @@
         def _():
             load_cot(k).wait()
 
-        @pl.loop(0, NODES_DEV // BLOCK)
+        @pl.loop(0, NODES_DEV // BLOCK, unroll=True)
         def _(i):
             at = pl.ds(pl.multiple_of(i * BLOCK, BLOCK), BLOCK)
             cot = cn[k, at, :].astype(F4)
@@ -325,7 +330,7 @@
 
         tmpn[...] = mm_nt(doutn[k], w_nout[...])
 
-        @pl.loop(0, NODES_DEV // BLOCK)
+        @pl.loop(0, NODES_DEV // BLOCK, unroll=True)
         def _(i):
             at = pl.ds(pl.multiple_of(i * BLOCK, BLOCK), BLOCK)
             dpren[k, at, :] = (tmpn[at, :] * silu_grad(pren[k, at, :])).astype(BF)
@@ -339,7 +344,7 @@
         tmp[...] = mm(inct[...], dagg[...])
         down[k] = cn[k].astype(F4) + mm_nt(dpren[k], w_nin[0:512])
 
-        @pl.loop(0, EDGES_DEV // BLOCK)
+        @pl.loop(0, EDGES_DEV // BLOCK, unroll=True)
         def _(i):
             at = pl.ds(pl.multiple_of(i * BLOCK, BLOCK), BLOCK)
             cot = tmp[at, :] + ce[k, at, :].astype(F4)

time: 91.3 us -> 76 us (0.83)
  Pallas kernels: 89 us -> 73.7 us
    pallas_call x1, Pallas kernels: 86.3 us -> 70.9 us  [layer_call(): pl.pallas_call(functools.partial(layer_kernel, nz=nz, factor=factor), out...]
where the time goes in v3:
time: 76 us; the launch traced here: 75 us
  Pallas kernels  73.7 us (97%)
  between operations  1.29 us (2%)
    pallas_call x1, Pallas kernels, layer_call(): pl.pallas_call(functools.partial(layer_kernel, nz=nz, factor=factor), out...  70.9 us
    pallas_call x1, Pallas kernels, finish_call(): pl.pallas_call(finish_kernel, out_shape=[jax.ShapeDtypeStruct((1, *node.s...  2.73 us

profile of v3, /device:TPU:2, one launch (start us, length us, event | category | flops | bytes accessed | tf_op | source)
XLA Modules:
  0.0 75.0 jit_solution(14823671253203999449)
XLA Ops:
  1.3 70.9 %layers.1 = (bf16[2,128,512]{2,1,0:T(8,128)(2,1)}, bf16[2,384,512]{2,1,0:T(8,128)(2,1)}, f32[4,32,128]{2,1,0:T(8,128)}) custom-call(s32[384]{0:T(512)} %src_in.1, s32[384]{0:T(512)} %dst_in.1, s32[1,4,16]{2,1,0:T(4,128)} %send_in.1, s32[1]{0:T(128)S(6)} %copy.21.count_in, bf16[2,128,512]{2,1,0:T(8,128)(2,1)} %node_in.1, bf16[2,384,512]{2,1,0:T(8,128)(2,1)} %edge_in.1, ...), custom_call_target="tpu_custom_call" | custom-call | tf_op jit(solution)/shard_map/layers/pallas_call | solution.py:608
  72.2 2.7 %finish.1 = (bf16[1,2,128,512]{3,2,1,0:T(8,128)(2,1)}, bf16[1,2,384,512]{3,2,1,0:T(8,128)(2,1)}, f32[12,1,512]{2,1,0:T(1,128)}, f32[1,4,512]{2,1,0:T(4,128)}, f3...) custom-call(bf16[2,128,512]{2,1,0:T(8,128)(2,1)} %get-tuple-element.19.node_in, ...), custom_call_target="tpu_custom_call" | custom-call | tf_op jit(solution)/shard_map/finish/pallas_call | solution.py:689

commit v4 on v3

--- a/solution.py
+++ b/solution.py
@@ -12,7 +12,6 @@
 EPS = 1e-05
 MESH = pl.DeviceIdType.MESH
 ROWS_A = 48
-ROWS_B = 64
 GAIN = 16
 NODES_DEV = 128
 EDGES_DEV = 384
@@ -27,10 +26,6 @@
     return jnp.dot(a, b, preferred_element_type=F4)
 
 
-def mm_nt(a, b):
-    return lax.dot_general(a, b, (((1,), (1,)), ((), ())), preferred_element_type=F4)
-
-
 def mm_tn(a, b):
     return lax.dot_general(a, b, (((0,), (0,)), ((), ())), preferred_element_type=F4)
 
@@ -45,14 +40,14 @@
     w_ein_in, w_eout_in, w_nin_in, w_nout_in, gain_e_in, gain_n_in,
     node_out, edge_out, fin_out,
     src_row, dst_row, send_row, count, w_ein, w_eout, w_nin, w_nout, gain_e, gain_n, l_first,
-    oht, oh, inc, inct, sendt, sendm,
+    t_ein, t_eout, t_nin, t_nout, oht, oh, inc, inct, sendt, sendm,
     tab, ein, cn, ce, cn32, halo1, halo2, hs1, hs2, bh,
     sr, pre, mid, tmp, xhat, rstd, enew, agg, pren, midn, tmpn, xhatn, rstdn, hnew,
     doutn, dpren, down, dagg, doute, dpre, gs, gr, de, dh, dge, dgn,
     s_halo1, s_halo2, r_halo, s_fe, r_fe, s_fh, r_fh,
     s_bh, r_bh1, r_bh2, s_be, r_be, s_bo, r_bo,
     l_node, l_edge, l_cot, l_nout, l_eout,
-    ga, gb, ta, ua, va, tb, ub, vb, a2, ta2, ua2, va2, b2, tb2, ub2, vb2, c3, rc3, fin, rfin,
+    ga, gb, ta, ua, va, tb, ub, vb, a2, ta2, ua2, va2, b2, tb2, ub2, vb2, ca, ra, cb, rb, fin,
     send_sem, recv_sem, l_fin,
     *, nz, factor,
 ):
@@ -80,7 +75,7 @@
         return {"dom": (dom // 2) * 2 + p % 2, "rep": p // 2}
 
     z_peers = [(z + j) % nz for j in range(1, nz)]
-    x_peers = [(px + j) % 4 for j in range(1, 4)]
+    x_peers = [(px + j) % 4 for j in (1, 3)]
     greet = [near(step, s) for step in OFFSETS for s in range(2)]
     greet += [at_y((y + 1) % 4), at_y((y + 3) % 4)]
     greet += [at_x(p) for p in x_peers] + [at_z(p) for p in z_peers]
@@ -328,21 +323,21 @@
             inv = rstdn[k, at, 0:1]
             doutn[k, at, :] = norm_back(cot, gain_n[...], hat, inv).astype(BF)
 
-        tmpn[...] = mm_nt(doutn[k], w_nout[...])
+        tmpn[...] = mm(doutn[k], t_nout[...])
 
         @pl.loop(0, NODES_DEV // BLOCK, unroll=True)
         def _(i):
             at = pl.ds(pl.multiple_of(i * BLOCK, BLOCK), BLOCK)
             dpren[k, at, :] = (tmpn[at, :] * silu_grad(pren[k, at, :])).astype(BF)
 
-        dagg[...] = mm_nt(dpren[k], w_nin[512:1024]).astype(BF)
+        dagg[...] = mm(dpren[k], t_nin[:, 512:1024]).astype(BF)
 
         @pl.when(first)
         def _():
             sib_de(k).wait_recv()
 
         tmp[...] = mm(inct[...], dagg[...])
-        down[k] = cn[k].astype(F4) + mm_nt(dpren[k], w_nin[0:512])
+        down[k] = cn[k].astype(F4) + mm(dpren[k], t_nin[:, 0:512])
 
         @pl.loop(0, EDGES_DEV // BLOCK, unroll=True)
         def _(i):
@@ -356,12 +351,12 @@
             inv = rstd[k, at, 0:1]
             doute[k, at, :] = norm_back(cot, gain_e[...], hat, inv).astype(BF)
 
-        grad = mm_nt(doute[k], w_eout[...])
+        grad = mm(doute[k], t_eout[...])
         pre[k] = grad * silu_grad(pre[k])
         dpre[k] = pre[k].astype(BF)
         gs[k] = mm(oht[0:TABLE], dpre[k]).astype(BF)
         gr[k] = mm(oht[TABLE:], dpre[k]).astype(BF)
-        bh[k] = mm_nt(gs[k, NODES_DEV:], w_ein[512:1024]).astype(BF)
+        bh[k] = mm(gs[k, NODES_DEV:], t_ein[:, 512:1024]).astype(BF)
 
         @pl.when(first)
         def _():
@@ -373,13 +368,13 @@
             for j in range(4):
                 back_copy(halo1, k, j, r_bh1).start()
 
-        down[k] += mm_nt(gs[k, 0:NODES_DEV], w_ein[512:1024]) + mm_nt(gr[k], w_ein[1024:1536])
+        down[k] += mm(gs[k, 0:NODES_DEV], t_ein[:, 512:1024]) + mm(gr[k], t_ein[:, 1024:1536])
 
         @pl.when(second)
         def _():
             sib_do(k).start()
 
-        de[k] = (tmp[...] + mm_nt(dpre[k], w_ein[0:512])).astype(BF)
+        de[k] = (tmp[...] + mm(dpre[k], t_ein[:, 0:512])).astype(BF)
 
         @pl.when(second)
         def _():
@@ -393,6 +388,15 @@
     def _(step):
         forward_now = (step == 0) | (step == 1 + seg)
         k = jnp.where(first, step % 2, step // 2)
+
+        @pl.when(step == 2 - 2 * seg)
+        def _():
+            for m in range(3):
+                t_ein[:, m * 512 : m * 512 + 512] = w_ein[m * 512 : m * 512 + 512].T
+            for m in range(2):
+                t_nin[:, m * 512 : m * 512 + 512] = w_nin[m * 512 : m * 512 + 512].T
+            t_eout[...] = w_eout[...].T
+            t_nout[...] = w_nout[...].T
 
         @pl.when(forward_now)
         def _():
@@ -408,12 +412,14 @@
             row = (r // 192) * ROWS_A + r % ROWS_A
             ga[(r % 192) // ROWS_A, row : row + 16, :] = value[q * 16 : q * 16 + 16].astype(BF)
 
-    def put_b(base, width, offset, value):
-        for q in range(128 // width):
-            zy = base // width + q
-            piece = value[q * width : (q + 1) * width].astype(BF)
-            for b in range(4):
-                gb[b, zy, offset : offset + width, :] = piece[:, b * 128 : (b + 1) * 128]
+    def put_b(m, n_lo, n_hi, e, o):
+        for q in range(8):
+            part = (n_lo, n_hi)[q // 4][q % 4 * 32 : q % 4 * 32 + 32]
+            for p in range(4):
+                b = p % 2 * 2 + p // 2
+                r = q * 16 + 4 * b
+                tile = jnp.concatenate([part[8 * b : 8 * b + 8], e[r : r + 4], o[r : r + 4]], axis=0)
+                gb[p, m * 8 + q] = tile.astype(BF)
 
     def both(ref):
         return ref[...].reshape(ref.shape[0] * ref.shape[1], ref.shape[2])
@@ -469,15 +475,18 @@
 
     ring_a = Ring(0, ga, ta, ua, va, y, at_y, 208)
     ring_b = Ring(6, gb, tb, ub, vb, px, at_x, 2 * nz)
-    ring_a2 = Ring(12, a2, ta2, ua2, va2, px, at_x, 208)
+    ring_a2 = Ring(12, a2, ta2, ua2, va2, px, at_x, nz // 2)
     ring_b2 = Ring(18, b2, tb2, ub2, vb2, y, at_y, nz // 2)
 
+    def nin_part(m):
+        lhs = own_cols(m) if m < 4 else cols(agg, m - 4)
+        return mm_tn(lhs, both(dpren))
+
     for m in range(4):
-        base = m * 128
-        put_b(base, 16, 48, mm_tn(cols(midn, m), both(doutn)))
-        put_b(base, 32, 0, mm_tn(own_cols(m), both(dpren)))
-        put_b(512 + base, 32, 0, mm_tn(cols(agg, m), both(dpren)))
-        put_b(base, 16, 32, mm_tn(cols(mid, m), both(doute)))
+        put_b(
+            m, nin_part(2 * m), nin_part(2 * m + 1),
+            mm_tn(cols(mid, m), both(doute)), mm_tn(cols(midn, m), both(doutn)),
+        )
     ring_b.start()
     for m in range(4):
         base = m * 128
@@ -501,15 +510,18 @@
             store_node(dh, k).start()
 
     ring_a.middle(16)
-    ring_b.middle(1)
+    ring_b.middle(2)
     ring_a.arrive()
-
-    @pl.loop(0, ga.shape[1] // 16)
+    gains = ring_a.total(slice(nz * ROWS_A, nz * ROWS_A + GAIN))[0:4]
+
+    @pl.loop(0, nz)
     def _(i):
-        at = pl.ds(pl.multiple_of(i * 16, 16), 16)
-        total = ring_a.total(at).astype(BF)
-        for b in range(4):
-            a2[b, at, :] = total[:, b * 128 : (b + 1) * 128]
+        at = pl.ds(pl.multiple_of(i * ROWS_A, 16), ROWS_A)
+        total = ring_a.total(at)
+        for p in range(4):
+            b = p % 2 * 2 + p // 2
+            tile = jnp.concatenate([total[12 * b : 12 * b + 12], gains], axis=0)
+            a2[p, i] = tile.astype(BF)
 
     ring_a2.start()
     ring_b.arrive()
@@ -520,51 +532,33 @@
             b2[q, i] = ring_b.total(i * 4 + q).astype(BF)
 
     ring_b2.start()
-    ring_a2.middle(16)
-    ring_b2.middle(1)
-    ring_a2.arrive()
-    gains = ring_a2.total(slice(nz * ROWS_A, nz * ROWS_A + GAIN)).astype(BF)
-
-    @pl.loop(0, nz)
-    def _(i):
-        at = pl.ds(pl.multiple_of(i * ROWS_A, 16), ROWS_A)
-        c3[i, 0:ROWS_A, :] = ring_a2.total(at).astype(BF)
-        c3[i, ROWS_A : ROWS_A + GAIN, :] = gains
-
-    ring_b2.arrive()
-
-    @pl.loop(0, nz)
-    def _(i):
-        c3[i, ROWS_A + GAIN :, :] = ring_b2.total(i).astype(BF)
-
-    third = [copy(24 + j, c3.at[p], rc3.at[j], at_z(p)) for j, p in enumerate(z_peers)]
-    for c in third:
-        c.start()
-    total = c3[z].astype(F4)
-    for j, c in enumerate(third):
-        c.wait_recv()
-        total = total + rc3[j].astype(F4)
-    total = total * factor
-
-    n0 = ROWS_A + GAIN
-    for p in range(4):
-        b = (p % 2) * 2 + p // 2
-        fin[p, 0:12, :] = total[12 * b : 12 * b + 12]
-        fin[p, 12:16, :] = total[n0 + 32 + 4 * b : n0 + 32 + 4 * b + 4]
-        fin[p, 16:24, :] = total[n0 + 8 * b : n0 + 8 * b + 8]
-        fin[p, 24:28, :] = total[n0 + 48 + 4 * b : n0 + 48 + 4 * b + 4]
-        fin[p, 28:32, :] = total[ROWS_A : ROWS_A + 4]
-    base = 24 + nz - 1
-    last = [copy(base + j, fin.at[p], rfin.at[px], at_x(p)) for j, p in enumerate(x_peers)]
-    for c in last:
-        c.start()
-    rfin[px] = fin[px]
-    for c in last:
-        c.wait_recv()
-    result = pltpu.make_async_copy(rfin, fin_out, l_fin.at[0])
+    ring_a2.middle(2)
+    ring_b2.middle(2)
+
+    def along_z(base, ring, held, got):
+        ring.arrive()
+        for i in range(nz):
+            held[i] = ring.total(i).astype(BF)
+        moves = [copy(base + j, held.at[p], got.at[j], at_z(p)) for j, p in enumerate(z_peers)]
+        for c in moves:
+            c.start()
+        return moves
+
+    def z_total(moves, held, got):
+        total = held[z].astype(F4)
+        for j, c in enumerate(moves):
+            c.wait_recv()
+            total = total + got[j].astype(F4)
+        return total * factor
+
+    third_a = along_z(24, ring_a2, ca, ra)
+    third_b = along_z(24 + nz - 1, ring_b2, cb, rb)
+    fin[0:16] = z_total(third_a, ca, ra)
+    fin[16:32] = z_total(third_b, cb, rb)
+    result = pltpu.make_async_copy(fin, fin_out, l_fin.at[0])
     result.start()
     result.wait()
-    for c in ring_a.out + ring_b.out + ring_a2.out + ring_b2.out + third + last:
+    for c in ring_a.out + ring_b.out + ring_a2.out + ring_b2.out + third_a + third_b:
         c.wait_send()
 
     @pl.when(first)
@@ -604,19 +598,20 @@
     dma = pltpu.SemaphoreType.DMA
     n, e = NODES_DEV, EDGES_DEV
     rows = nz * ROWS_A + GAIN
-    copies = 24 + nz - 1 + 3
+    copies = 24 + 2 * (nz - 1)
     return pl.pallas_call(
         functools.partial(layer_kernel, nz=nz, factor=factor),
         out_shape=[
             jax.ShapeDtypeStruct((2, n, 512), BF),
             jax.ShapeDtypeStruct((2, e, 512), BF),
-            jax.ShapeDtypeStruct((4, 32, 128), F4),
+            jax.ShapeDtypeStruct((32, 512), F4),
         ],
         in_specs=[hbm] * 13,
         out_specs=[hbm] * 3,
         scratch_shapes=[
             pltpu.VMEM((e,), i32), pltpu.VMEM((e,), i32), pltpu.VMEM((1, 4, HALO), i32), pltpu.SMEM((1,), i32),
             bf(1536, 512), bf(512, 512), bf(1024, 512), bf(512, 512), fl(1, 512), fl(1, 512), dma((10,)),
+            bf(512, 1536), bf(512, 512), bf(512, 1024), bf(512, 512),
             bf(320, e), bf(e, 320), bf(n, e), bf(e, n), bf(n, n), bf(n, n),
             bf(2, TABLE, 512), bf(2, e, 512), bf(2, n, 512), bf(2, e, 512), fl(2, n, 512),
             bf(2, HALOS, 512), bf(2, HALOS, 512), bf(2, HALOS, 512), bf(2, HALOS, 512), bf(2, HALOS, 512),
@@ -628,12 +623,12 @@
             dma((2, 4)), dma((2, 4)), dma((2, 4)), dma((2,)), dma((2,)), dma((2,)), dma((2,)),
             dma((2, 4)), dma((2, 4)), dma((2, 4)), dma((2,)), dma((2,)), dma((2,)), dma((2,)),
             dma((2,)), dma((2,)), dma((2,)), dma((2,)), dma((2,)),
-            bf(4, rows, 512), bf(4, 4 * nz, ROWS_B, 128),
+            bf(4, rows, 512), bf(4, 4 * nz, 16, 512),
             bf(rows, 512), bf(rows, 512), bf(rows, 512),
-            bf(4 * nz, ROWS_B, 128), bf(4 * nz, ROWS_B, 128), bf(4 * nz, ROWS_B, 128),
-            bf(4, rows, 128), bf(rows, 128), bf(rows, 128), bf(rows, 128),
-            bf(4, nz, ROWS_B, 128), bf(nz, ROWS_B, 128), bf(nz, ROWS_B, 128), bf(nz, ROWS_B, 128),
-            bf(nz, 128, 128), bf(nz - 1, 128, 128), fl(4, 32, 128), fl(4, 32, 128),
+            bf(4 * nz, 16, 512), bf(4 * nz, 16, 512), bf(4 * nz, 16, 512),
+            bf(4, nz, 16, 512), bf(nz, 16, 512), bf(nz, 16, 512), bf(nz, 16, 512),
+            bf(4, nz, 16, 512), bf(nz, 16, 512), bf(nz, 16, 512), bf(nz, 16, 512),
+            bf(nz, 16, 512), bf(nz - 1, 16, 512), bf(nz, 16, 512), bf(nz - 1, 16, 512), fl(32, 512),
             dma((copies,)), dma((copies,)), dma((1,)),
         ],
         compiler_params=pltpu.CompilerParams(
@@ -663,20 +658,18 @@
         w.start()
     first.wait()
     t = lax.axis_index("dom") * 2 + lax.axis_index("rep")
-    lane = lax.broadcasted_iota(jnp.int32, (2, 128), 1)
+    for r in range(12):
+        ein_o[r] = rfin[r : r + 1]
+    nin_o[0] = rfin[16:24]
+    eout_o[0] = rfin[24:28]
+    nout_o[0] = rfin[28:32]
+    pair = rfin[12:14]
+    lane = lax.broadcasted_iota(jnp.int32, (2, 512), 1)
+    narrow = lax.broadcasted_iota(jnp.int32, (2, 128), 1)
     picked = jnp.zeros((2, 128), F4)
-    for b in range(4):
-        at = slice(b * 128, (b + 1) * 128)
-        for r in range(12):
-            ein_o[r, :, at] = rfin[b, r : r + 1, :]
-        eout_o[0, :, at] = rfin[b, 12:16, :]
-        nin_o[0, :, at] = rfin[b, 16:24, :]
-        nout_o[0, :, at] = rfin[b, 24:28, :]
-        pair = rfin[b, 28:30, :]
-        for i in range(4):
-            hit = jnp.where(lane + b * 128 == t * 4 + i, pair, 0.0)
-            value = jnp.sum(hit, axis=1, keepdims=True)
-            picked = picked + jnp.where(lane == i, value, 0.0)
+    for i in range(4):
+        value = jnp.sum(jnp.where(lane == t * 4 + i, pair, 0.0), axis=1, keepdims=True)
+        picked = picked + jnp.where(narrow == i, value, 0.0)
     ge_o[...] = picked[0:1, 0:4]
     gn_o[...] = picked[1:2, 0:4]
     for c in stores:
@@ -701,7 +694,7 @@
         in_specs=[hbm] * 3,
         out_specs=[hbm] * 2 + [vm] * 6,
         scratch_shapes=[
-            pltpu.VMEM((4, 32, 128), F4), pltpu.VMEM(node.shape, BF), pltpu.VMEM(edge.shape, BF),
+            pltpu.VMEM((32, 512), F4), pltpu.VMEM(node.shape, BF), pltpu.VMEM(edge.shape, BF),
             pltpu.SemaphoreType.DMA((7,)), pltpu.SemaphoreType.DMA((6,)),
         ],
         compiler_params=pltpu.CompilerParams(vmem_limit_bytes=56 << 20),

time: 76 us -> 71.4 us (0.939); the launches traced: 75 us -> 71.1 us
  Pallas kernels: 73.7 us -> 69.8 us
    pallas_call x1, Pallas kernels: 70.9 us -> 67.1 us  [layer_call(): pl.pallas_call(functools.partial(layer_kernel, nz=nz, factor=factor), out...]
where the time goes in v4:
time: 71.4 us; the launch traced here: 71.1 us
  Pallas kernels  69.8 us (98%)
  between operations  1.29 us (2%)
    pallas_call x1, Pallas kernels, layer_call(): pl.pallas_call(functools.partial(layer_kernel, nz=nz, factor=factor), out...  67.1 us
    pallas_call x1, Pallas kernels, finish_call(): pl.pallas_call(finish_kernel, out_shape=[jax.ShapeDtypeStruct((1, *node.s...  2.73 us

profile of v4, /device:TPU:2, one launch (start us, length us, event | category | flops | bytes accessed | tf_op | source)
XLA Modules:
  0.0 71.1 jit_solution(16067320453492800140)
XLA Ops:
  1.3 67.1 %layers.1 = (bf16[2,128,512]{2,1,0:T(8,128)(2,1)}, bf16[2,384,512]{2,1,0:T(8,128)(2,1)}, f32[32,512]{1,0:T(8,128)}) custom-call(s32[384]{0:T(512)} %src_in.1, s32[384]{0:T(512)} %dst_in.1, s32[1,4,16]{2,1,0:T(4,128)} %send_in.1, s32[1]{0:T(128)S(6)} %copy.21.count_in, bf16[2,128,512]{2,1,0:T(8,128)(2,1)} %node_in.1, bf16[2,384,512]{2,1,0:T(8,128)(2,1)} %edge_in.1, ...), custom_call_target="tpu_custom_call" | custom-call | tf_op jit(solution)/shard_map/layers/pallas_call | solution.py:602
  68.4 2.7 %finish.1 = (bf16[1,2,128,512]{3,2,1,0:T(8,128)(2,1)}, bf16[1,2,384,512]{3,2,1,0:T(8,128)(2,1)}, f32[12,1,512]{2,1,0:T(1,128)}, f32[1,4,512]{2,1,0:T(4,128)}, f3...) custom-call(bf16[2,128,512]{2,1,0:T(8,128)(2,1)} %get-tuple-element.19.node_in, ...), custom_call_target="tpu_custom_call" | custom-call | tf_op jit(solution)/shard_map/finish/pallas_call | solution.py:682

commit v5 on v4

--- a/solution.py
+++ b/solution.py
@@ -13,6 +13,7 @@
 MESH = pl.DeviceIdType.MESH
 ROWS_A = 48
 GAIN = 16
+LANES = 384
 NODES_DEV = 128
 EDGES_DEV = 384
 HALOS = 64
@@ -47,7 +48,7 @@
     s_halo1, s_halo2, r_halo, s_fe, r_fe, s_fh, r_fh,
     s_bh, r_bh1, r_bh2, s_be, r_be, s_bo, r_bo,
     l_node, l_edge, l_cot, l_nout, l_eout,
-    ga, gb, ta, ua, va, tb, ub, vb, a2, ta2, ua2, va2, b2, tb2, ub2, vb2, ca, ra, cb, rb, fin,
+    ga, gb, ta, ua, va, tb, ub, vb, a2, ta2, ua2, va2, b2, tb2, ub2, vb2, ca, ra, cb, rb, fin, gz, zr, zl, hy, ry, hx, rx,
     send_sem, recv_sem, l_fin,
     *, nz, factor,
 ):
@@ -75,10 +76,10 @@
         return {"dom": (dom // 2) * 2 + p % 2, "rep": p // 2}
 
     z_peers = [(z + j) % nz for j in range(1, nz)]
-    x_peers = [(px + j) % 4 for j in (1, 3)]
+    x_peers = [(px + j) % 4 for j in range(1, 4)]
+    y_peers = [(y + j) % 4 for j in range(1, 4)]
     greet = [near(step, s) for step in OFFSETS for s in range(2)]
-    greet += [at_y((y + 1) % 4), at_y((y + 3) % 4)]
-    greet += [at_x(p) for p in x_peers] + [at_z(p) for p in z_peers]
+    greet += [at_y(p) for p in y_peers] + [at_x(p) for p in x_peers] + [at_z(p) for p in z_peers]
     greet += [{"segment": 1 - seg}]
     barrier = pltpu.get_barrier_semaphore()
     for device in greet:
@@ -199,8 +200,10 @@
     oht[0:TABLE] = f_src.astype(BF)
     oht[TABLE:] = f_dst.astype(BF)
     inc[...] = f_inc.astype(BF)
-    oh[:, 0:TABLE] = f_src.T.astype(BF)
-    oh[:, TABLE:] = f_dst.T.astype(BF)
+    t_src = f_src.T.astype(BF)
+    oh[:, 0:NODES_DEV] = t_src[:, 0:NODES_DEV]
+    oh[:, NODES_DEV : 2 * NODES_DEV] = f_dst.T.astype(BF)
+    oh[:, 2 * NODES_DEV :] = t_src[:, NODES_DEV:]
     inct[...] = f_inc.T.astype(BF)
     dge[...] = jnp.zeros_like(dge)
     dgn[...] = jnp.zeros_like(dgn)
@@ -243,11 +246,13 @@
             sib_h(k).wait_recv()
 
         own = tab[k, 0:NODES_DEV]
-        sr[TABLE:] = mm(own, w_ein[1024:1536]).astype(BF)
+        sr[0:NODES_DEV] = mm(own, w_ein[512:1024]).astype(BF)
+        sr[NODES_DEV : 2 * NODES_DEV] = mm(own, w_ein[1024:1536]).astype(BF)
+        pre[k] += mm(oh[:, 0 : 2 * NODES_DEV], sr[0 : 2 * NODES_DEV])
         for j in range(4):
             halo_copy(hs1, k, j, s_halo1, 0).wait_recv()
-        sr[0:TABLE] = mm(tab[k], w_ein[512:1024]).astype(BF)
-        tmp[...] = mm(oh[...], sr[...])
+        sr[2 * NODES_DEV :] = mm(tab[k, NODES_DEV:], w_ein[512:1024]).astype(BF)
+        tmp[...] = mm(oh[:, 2 * NODES_DEV :], sr[2 * NODES_DEV :])
 
         @pl.loop(0, EDGES_DEV // BLOCK, unroll=True)
         def _(i):
@@ -293,10 +298,10 @@
 
         @pl.when(first)
         def _():
-            sib_h(k).start()
             hs2[k] = mm(sendm[0:HALOS], hnew[k]).astype(BF)
             for j in range(4):
                 halo_copy(hs2, k, j, s_halo2, 1).start()
+            sib_h(k).start()
 
         @pl.when(second)
         def _():
@@ -419,7 +424,8 @@
                 b = p % 2 * 2 + p // 2
                 r = q * 16 + 4 * b
                 tile = jnp.concatenate([part[8 * b : 8 * b + 8], e[r : r + 4], o[r : r + 4]], axis=0)
-                gb[p, m * 8 + q] = tile.astype(BF)
+                gb[p, m * 8 + q] = tile[:, 0:LANES].astype(BF)
+                gz[2 * m + q // 4, q % 4, p] = tile[:, LANES:].astype(BF)
 
     def both(ref):
         return ref[...].reshape(ref.shape[0] * ref.shape[1], ref.shape[2])
@@ -488,6 +494,24 @@
             mm_tn(cols(mid, m), both(doute)), mm_tn(cols(midn, m), both(doutn)),
         )
     ring_b.start()
+    zc = 24 + 2 * (nz - 1)
+    up, low = at_z((z + 1) % nz), at_z((z + nz - 1) % nz)
+    flow_up = [copy(zc, gz.at[(z + 4) % nz], zr.at[0], up)]
+    flow_up += [copy(zc + 1 + i, zr.at[i], zr.at[i + 1], up) for i in range(3)]
+    flow_low = [copy(zc + 4, gz.at[(z + nz - 3) % nz], zl.at[0], low)]
+    flow_low += [copy(zc + 5 + i, zl.at[i], zl.at[i + 1], low) for i in range(2)]
+    flow_up[0].start()
+    flow_low[0].start()
+
+    def pass_on(i):
+        for flow, held, q in ((flow_up, zr, z + 3 - i), (flow_low, zl, z + nz - 2 + i)):
+            if i + 1 < len(flow):
+                flow[i].wait_recv()
+                for r in range(4):
+                    part = held[i, r].astype(F4) + gz[q % nz, r].astype(F4)
+                    held[i, r] = part.astype(BF)
+                flow[i + 1].start()
+
     for m in range(4):
         base = m * 128
         put_ein(base, mm_tn(cols(ein, m), both(dpre)))
@@ -509,8 +533,19 @@
             dh[k] = (down[k] + mm(sendt[:, 0:HALOS], halo2[k])).astype(BF)
             store_node(dh, k).start()
 
+    pass_on(0)
+    pass_on(1)
+    pass_on(2)
     ring_a.middle(16)
     ring_b.middle(2)
+    flow_up[3].wait_recv()
+    flow_low[2].wait_recv()
+    for r in range(4):
+        part = gz[z, r].astype(F4) + zr[3, r].astype(F4) + zl[2, r].astype(F4)
+        hy[r] = part.astype(BF)
+    flow_y = [copy(zc + 7 + j, hy.at[p], ry.at[j], at_y(p)) for j, p in enumerate(y_peers)]
+    for c in flow_y:
+        c.start()
     ring_a.arrive()
     gains = ring_a.total(slice(nz * ROWS_A, nz * ROWS_A + GAIN))[0:4]
 
@@ -532,6 +567,14 @@
             b2[q, i] = ring_b.total(i * 4 + q).astype(BF)
 
     ring_b2.start()
+    part = hy[y].astype(F4)
+    for j, c in enumerate(flow_y):
+        c.wait_recv()
+        part = part + ry[j].astype(F4)
+    hx[...] = part.astype(BF)
+    flow_x = [copy(zc + 10 + j, hx.at[p], rx.at[j], at_x(p)) for j, p in enumerate(x_peers)]
+    for c in flow_x:
+        c.start()
     ring_a2.middle(2)
     ring_b2.middle(2)
 
@@ -553,12 +596,17 @@
 
     third_a = along_z(24, ring_a2, ca, ra)
     third_b = along_z(24 + nz - 1, ring_b2, cb, rb)
+    part = hx[px].astype(F4)
+    for j, c in enumerate(flow_x):
+        c.wait_recv()
+        part = part + rx[j].astype(F4)
+    fin[16:32, LANES:] = part * factor
     fin[0:16] = z_total(third_a, ca, ra)
-    fin[16:32] = z_total(third_b, cb, rb)
+    fin[16:32, 0:LANES] = z_total(third_b, cb, rb)
     result = pltpu.make_async_copy(fin, fin_out, l_fin.at[0])
     result.start()
     result.wait()
-    for c in ring_a.out + ring_b.out + ring_a2.out + ring_b2.out + third_a + third_b:
+    for c in ring_a.out + ring_b.out + ring_a2.out + ring_b2.out + third_a + third_b + flow_up + flow_low + flow_y + flow_x:
         c.wait_send()
 
     @pl.when(first)
@@ -598,7 +646,7 @@
     dma = pltpu.SemaphoreType.DMA
     n, e = NODES_DEV, EDGES_DEV
     rows = nz * ROWS_A + GAIN
-    copies = 24 + 2 * (nz - 1)
+    copies = 24 + 2 * (nz - 1) + 13
     return pl.pallas_call(
         functools.partial(layer_kernel, nz=nz, factor=factor),
         out_shape=[
@@ -623,12 +671,14 @@
             dma((2, 4)), dma((2, 4)), dma((2, 4)), dma((2,)), dma((2,)), dma((2,)), dma((2,)),
             dma((2, 4)), dma((2, 4)), dma((2, 4)), dma((2,)), dma((2,)), dma((2,)), dma((2,)),
             dma((2,)), dma((2,)), dma((2,)), dma((2,)), dma((2,)),
-            bf(4, rows, 512), bf(4, 4 * nz, 16, 512),
+            bf(4, rows, 512), bf(4, 4 * nz, 16, LANES),
             bf(rows, 512), bf(rows, 512), bf(rows, 512),
-            bf(4 * nz, 16, 512), bf(4 * nz, 16, 512), bf(4 * nz, 16, 512),
+            bf(4 * nz, 16, LANES), bf(4 * nz, 16, LANES), bf(4 * nz, 16, LANES),
             bf(4, nz, 16, 512), bf(nz, 16, 512), bf(nz, 16, 512), bf(nz, 16, 512),
-            bf(4, nz, 16, 512), bf(nz, 16, 512), bf(nz, 16, 512), bf(nz, 16, 512),
-            bf(nz, 16, 512), bf(nz - 1, 16, 512), bf(nz, 16, 512), bf(nz - 1, 16, 512), fl(32, 512),
+            bf(4, nz, 16, LANES), bf(nz, 16, LANES), bf(nz, 16, LANES), bf(nz, 16, LANES),
+            bf(nz, 16, 512), bf(nz - 1, 16, 512), bf(nz, 16, LANES), bf(nz - 1, 16, LANES), fl(32, 512),
+            bf(nz, 4, 4, 16, 128), bf(4, 4, 4, 16, 128), bf(3, 4, 4, 16, 128),
+            bf(4, 4, 16, 128), bf(3, 4, 16, 128), bf(4, 16, 128), bf(3, 16, 128),
             dma((copies,)), dma((copies,)), dma((1,)),
         ],
         compiler_params=pltpu.CompilerParams(

time: 71.4 us -> 74.2 us (1.039)
  Pallas kernels: 69.8 us -> 72.4 us
    pallas_call x1, Pallas kernels: 67.1 us -> 69.7 us  [layer_call(): pl.pallas_call(functools.partial(layer_kernel, nz=nz, factor=factor), out...]
where the time goes in v5:
time: 74.2 us; the launch traced here: 73.7 us
  Pallas kernels  72.4 us (98%)
  between operations  1.29 us (2%)
    pallas_call x1, Pallas kernels, layer_call(): pl.pallas_call(functools.partial(layer_kernel, nz=nz, factor=factor), out...  69.7 us
    pallas_call x1, Pallas kernels, finish_call(): pl.pallas_call(finish_kernel, out_shape=[jax.ShapeDtypeStruct((1, *node.s...  2.73 us

profile of v5, /device:TPU:2, one launch (start us, length us, event | category | flops | bytes accessed | tf_op | source)
XLA Modules:
  0.0 73.7 jit_solution(6975069801232587704)
XLA Ops:
  1.3 69.7 %layers.1 = (bf16[2,128,512]{2,1,0:T(8,128)(2,1)}, bf16[2,384,512]{2,1,0:T(8,128)(2,1)}, f32[32,512]{1,0:T(8,128)}) custom-call(s32[384]{0:T(512)} %src_in.1, s32[384]{0:T(512)} %dst_in.1, s32[1,4,16]{2,1,0:T(4,128)} %send_in.1, s32[1]{0:T(128)S(6)} %copy.21.count_in, bf16[2,128,512]{2,1,0:T(8,128)(2,1)} %node_in.1, bf16[2,384,512]{2,1,0:T(8,128)(2,1)} %edge_in.1, ...), custom_call_target="tpu_custom_call" | custom-call | tf_op jit(solution)/shard_map/layers/pallas_call | solution.py:650
  71.0 2.7 %finish.1 = (bf16[1,2,128,512]{3,2,1,0:T(8,128)(2,1)}, bf16[1,2,384,512]{3,2,1,0:T(8,128)(2,1)}, f32[12,1,512]{2,1,0:T(1,128)}, f32[1,4,512]{2,1,0:T(4,128)}, f3...) custom-call(bf16[2,128,512]{2,1,0:T(8,128)(2,1)} %get-tuple-element.19.node_in, ...), custom_call_target="tpu_custom_call" | custom-call | tf_op jit(solution)/shard_map/finish/pallas_call | solution.py:732

commit v6 on v5

--- a/solution.py
+++ b/solution.py
@@ -48,7 +48,7 @@
     s_halo1, s_halo2, r_halo, s_fe, r_fe, s_fh, r_fh,
     s_bh, r_bh1, r_bh2, s_be, r_be, s_bo, r_bo,
     l_node, l_edge, l_cot, l_nout, l_eout,
-    ga, gb, ta, ua, va, tb, ub, vb, a2, ta2, ua2, va2, b2, tb2, ub2, vb2, ca, ra, cb, rb, fin, gz, zr, zl, hy, ry, hx, rx,
+    ga, gb, ta, ua, va, tb, ub, vb, a2, ga2, b2, gb2, ca, ra, cb, rb, fin, gz, zr, zl, hy, ry, hx, rx,
     send_sem, recv_sem, l_fin,
     *, nz, factor,
 ):
@@ -464,7 +464,7 @@
             for c, q, lo, hi in ((0, self.right, 0, cut), (1, self.left, cut, n)):
                 self.out[c].wait_recv()
 
-                @pl.loop(lo // block, hi // block)
+                @pl.loop(lo // block, hi // block, unroll=4 if (hi - lo) // block % 4 == 0 else 1)
                 def _(i):
                     at = pl.ds(pl.multiple_of(i * block, block), block)
                     t[at] = (t[at].astype(F4) + src[q, at].astype(F4)).astype(BF)
@@ -481,8 +481,11 @@
 
     ring_a = Ring(0, ga, ta, ua, va, y, at_y, 208)
     ring_b = Ring(6, gb, tb, ub, vb, px, at_x, 2 * nz)
-    ring_a2 = Ring(12, a2, ta2, ua2, va2, px, at_x, nz // 2)
-    ring_b2 = Ring(18, b2, tb2, ub2, vb2, y, at_y, nz // 2)
+    def spread(base, src, got, peers, at):
+        moves = [copy(base + j, src.at[p], got.at[j], at(p)) for j, p in enumerate(peers)]
+        for c in moves:
+            c.start()
+        return moves
 
     def nin_part(m):
         lhs = own_cols(m) if m < 4 else cols(agg, m - 4)
@@ -535,21 +538,19 @@
 
     pass_on(0)
     pass_on(1)
+    ring_b.middle(2)
+    ring_a.middle(16)
     pass_on(2)
-    ring_a.middle(16)
-    ring_b.middle(2)
     flow_up[3].wait_recv()
     flow_low[2].wait_recv()
     for r in range(4):
         part = gz[z, r].astype(F4) + zr[3, r].astype(F4) + zl[2, r].astype(F4)
         hy[r] = part.astype(BF)
-    flow_y = [copy(zc + 7 + j, hy.at[p], ry.at[j], at_y(p)) for j, p in enumerate(y_peers)]
-    for c in flow_y:
-        c.start()
+    flow_y = spread(zc + 7, hy, ry, y_peers, at_y)
     ring_a.arrive()
     gains = ring_a.total(slice(nz * ROWS_A, nz * ROWS_A + GAIN))[0:4]
 
-    @pl.loop(0, nz)
+    @pl.loop(0, nz, unroll=4)
     def _(i):
         at = pl.ds(pl.multiple_of(i * ROWS_A, 16), ROWS_A)
         total = ring_a.total(at)
@@ -558,34 +559,31 @@
             tile = jnp.concatenate([total[12 * b : 12 * b + 12], gains], axis=0)
             a2[p, i] = tile.astype(BF)
 
-    ring_a2.start()
+    second_a = spread(12, a2, ga2, x_peers, at_x)
     ring_b.arrive()
 
-    @pl.loop(0, nz)
+    @pl.loop(0, nz, unroll=4)
     def _(i):
         for q in range(4):
             b2[q, i] = ring_b.total(i * 4 + q).astype(BF)
 
-    ring_b2.start()
+    second_b = spread(15, b2, gb2, y_peers, at_y)
     part = hy[y].astype(F4)
     for j, c in enumerate(flow_y):
         c.wait_recv()
         part = part + ry[j].astype(F4)
     hx[...] = part.astype(BF)
-    flow_x = [copy(zc + 10 + j, hx.at[p], rx.at[j], at_x(p)) for j, p in enumerate(x_peers)]
-    for c in flow_x:
-        c.start()
-    ring_a2.middle(2)
-    ring_b2.middle(2)
-
-    def along_z(base, ring, held, got):
-        ring.arrive()
+    flow_x = spread(zc + 10, hx, rx, x_peers, at_x)
+
+    def along_z(base, moves, src, got, me, held, into):
+        for c in moves:
+            c.wait_recv()
         for i in range(nz):
-            held[i] = ring.total(i).astype(BF)
-        moves = [copy(base + j, held.at[p], got.at[j], at_z(p)) for j, p in enumerate(z_peers)]
-        for c in moves:
-            c.start()
-        return moves
+            total = src[me, i].astype(F4)
+            for j in range(3):
+                total = total + got[j, i].astype(F4)
+            held[i] = total.astype(BF)
+        return spread(base, held, into, z_peers, at_z)
 
     def z_total(moves, held, got):
         total = held[z].astype(F4)
@@ -594,8 +592,8 @@
             total = total + got[j].astype(F4)
         return total * factor
 
-    third_a = along_z(24, ring_a2, ca, ra)
-    third_b = along_z(24 + nz - 1, ring_b2, cb, rb)
+    third_a = along_z(24, second_a, a2, ga2, px, ca, ra)
+    third_b = along_z(24 + nz - 1, second_b, b2, gb2, y, cb, rb)
     part = hx[px].astype(F4)
     for j, c in enumerate(flow_x):
         c.wait_recv()
@@ -606,7 +604,7 @@
     result = pltpu.make_async_copy(fin, fin_out, l_fin.at[0])
     result.start()
     result.wait()
-    for c in ring_a.out + ring_b.out + ring_a2.out + ring_b2.out + third_a + third_b + flow_up + flow_low + flow_y + flow_x:
+    for c in ring_a.out + ring_b.out + second_a + second_b + third_a + third_b + flow_up + flow_low + flow_y + flow_x:
         c.wait_send()
 
     @pl.when(first)
@@ -674,8 +672,8 @@
             bf(4, rows, 512), bf(4, 4 * nz, 16, LANES),
             bf(rows, 512), bf(rows, 512), bf(rows, 512),
             bf(4 * nz, 16, LANES), bf(4 * nz, 16, LANES), bf(4 * nz, 16, LANES),
-            bf(4, nz, 16, 512), bf(nz, 16, 512), bf(nz, 16, 512), bf(nz, 16, 512),
-            bf(4, nz, 16, LANES), bf(nz, 16, LANES), bf(nz, 16, LANES), bf(nz, 16, LANES),
+            bf(4, nz, 16, 512), bf(3, nz, 16, 512),
+            bf(4, nz, 16, LANES), bf(3, nz, 16, LANES),
             bf(nz, 16, 512), bf(nz - 1, 16, 512), bf(nz, 16, LANES), bf(nz - 1, 16, LANES), fl(32, 512),
             bf(nz, 4, 4, 16, 128), bf(4, 4, 4, 16, 128), bf(3, 4, 4, 16, 128),
             bf(4, 4, 16, 128), bf(3, 4, 16, 128), bf(4, 16, 128), bf(3, 16, 128),

time: 74.2 us -> 70.9 us (0.956); the launches traced: 73.7 us -> 69.6 us
  Pallas kernels: 72.4 us -> 68.3 us
    pallas_call x1, Pallas kernels: 69.7 us -> 65.5 us  [layer_call(): pl.pallas_call(functools.partial(layer_kernel, nz=nz, factor=factor), out...]
where the time goes in v6:
time: 70.9 us; the launch traced here: 69.6 us
  Pallas kernels  68.3 us (96%)
  between operations  1.29 us (2%)
    pallas_call x1, Pallas kernels, layer_call(): pl.pallas_call(functools.partial(layer_kernel, nz=nz, factor=factor), out...  65.5 us
    pallas_call x1, Pallas kernels, finish_call(): pl.pallas_call(finish_kernel, out_shape=[jax.ShapeDtypeStruct((1, *node.s...  2.73 us

profile of v6, /device:TPU:2, one launch (start us, length us, event | category | flops | bytes accessed | tf_op | source)
XLA Modules:
  0.0 69.6 jit_solution(3988766438104623092)
XLA Ops:
  1.3 65.5 %layers.1 = (bf16[2,128,512]{2,1,0:T(8,128)(2,1)}, bf16[2,384,512]{2,1,0:T(8,128)(2,1)}, f32[32,512]{1,0:T(8,128)}) custom-call(s32[384]{0:T(512)} %src_in.1, s32[384]{0:T(512)} %dst_in.1, s32[1,4,16]{2,1,0:T(4,128)} %send_in.1, s32[1]{0:T(128)S(6)} %copy.21.count_in, bf16[2,128,512]{2,1,0:T(8,128)(2,1)} %node_in.1, bf16[2,384,512]{2,1,0:T(8,128)(2,1)} %edge_in.1, ...), custom_call_target="tpu_custom_call" | custom-call | tf_op jit(solution)/shard_map/layers/pallas_call | solution.py:648
  66.8 2.7 %finish.1 = (bf16[1,2,128,512]{3,2,1,0:T(8,128)(2,1)}, bf16[1,2,384,512]{3,2,1,0:T(8,128)(2,1)}, f32[12,1,512]{2,1,0:T(1,128)}, f32[1,4,512]{2,1,0:T(4,128)}, f3...) custom-call(bf16[2,128,512]{2,1,0:T(8,128)(2,1)} %get-tuple-element.19.node_in, ...), custom_call_target="tpu_custom_call" | custom-call | tf_op jit(solution)/shard_map/finish/pallas_call | solution.py:730

commit v7 on v6

--- a/solution.py
+++ b/solution.py
@@ -48,8 +48,8 @@
     s_halo1, s_halo2, r_halo, s_fe, r_fe, s_fh, r_fh,
     s_bh, r_bh1, r_bh2, s_be, r_be, s_bo, r_bo,
     l_node, l_edge, l_cot, l_nout, l_eout,
-    ga, gb, ta, ua, va, tb, ub, vb, a2, ga2, b2, gb2, ca, ra, cb, rb, fin, gz, zr, zl, hy, ry, hx, rx,
-    send_sem, recv_sem, l_fin,
+    ga, gb, ta, ua, va, tb, ub, vb, a2, ga2, b2, gb2, ca, ra, cb, rb, gz, zr, zl, hy, ry, hx, rx,
+    send_sem, recv_sem,
     *, nz, factor,
 ):
     seg = lax.axis_index("segment")
@@ -81,59 +81,8 @@
     greet = [near(step, s) for step in OFFSETS for s in range(2)]
     greet += [at_y(p) for p in y_peers] + [at_x(p) for p in x_peers] + [at_z(p) for p in z_peers]
     greet += [{"segment": 1 - seg}]
-    barrier = pltpu.get_barrier_semaphore()
-    for device in greet:
-        pl.semaphore_signal(barrier, inc=1, device_id=device, device_id_type=MESH)
-
-    def remote(src, dst, send, recv, device):
-        return pltpu.make_async_remote_copy(
-            src_ref=src, dst_ref=dst, send_sem=send, recv_sem=recv,
-            device_id=device, device_id_type=MESH,
-        )
-
     def load_node(k):
         return pltpu.make_async_copy(node_in.at[k], tab.at[k, 0:NODES_DEV], l_node.at[k])
-
-    def load_edge(k):
-        return pltpu.make_async_copy(edge_in.at[k], ein.at[k], l_edge.at[k])
-
-    def load_cot(k):
-        return pltpu.make_async_copy(cot_in.at[k], cn.at[k], l_cot.at[k])
-
-    def store_node(src, k):
-        return pltpu.make_async_copy(src.at[k], node_out.at[k], l_nout.at[k])
-
-    def store_edge(src, k):
-        return pltpu.make_async_copy(src.at[k], edge_out.at[k], l_eout.at[k])
-
-    def halo_copy(src, k, j, sems, segment):
-        rows = slice(j * HALO, (j + 1) * HALO)
-        into = slice(NODES_DEV + j * HALO, NODES_DEV + (j + 1) * HALO)
-        return remote(
-            src.at[k, rows], tab.at[k, into], sems.at[k, j], r_halo.at[k, j],
-            near(OFFSETS[j], segment),
-        )
-
-    def back_copy(dst, k, j, recv):
-        rows = slice(j * HALO, (j + 1) * HALO)
-        return remote(
-            bh.at[k, rows], dst.at[k, rows], s_bh.at[k, j], recv.at[k, j],
-            near(-OFFSETS[j], 0),
-        )
-
-    def sib_e(k):
-        return remote(enew.at[k], ein.at[k], s_fe.at[k], r_fe.at[k], {"segment": 1 - seg})
-
-    def sib_h(k):
-        return remote(
-            hnew.at[k], tab.at[k, 0:NODES_DEV], s_fh.at[k], r_fh.at[k], {"segment": 1 - seg}
-        )
-
-    def sib_de(k):
-        return remote(de.at[k], ce.at[k], s_be.at[k], r_be.at[k], {"segment": 1 - seg})
-
-    def sib_do(k):
-        return remote(down.at[k], cn32.at[k], s_bo.at[k], r_bo.at[k], {"segment": 1 - seg})
 
     small = [
         pltpu.make_async_copy(u, v, l_first.at[i])
@@ -144,19 +93,74 @@
             ]
         )
     ]
+    for c in small:
+        c.start()
+
+    @pl.when(first)
+    def _():
+        for k in range(2):
+            load_node(k).start()
+
+    barrier = pltpu.get_barrier_semaphore()
+    for device in greet:
+        pl.semaphore_signal(barrier, inc=1, device_id=device, device_id_type=MESH)
+
+    def remote(src, dst, send, recv, device):
+        return pltpu.make_async_remote_copy(
+            src_ref=src, dst_ref=dst, send_sem=send, recv_sem=recv,
+            device_id=device, device_id_type=MESH,
+        )
+
+    def load_edge(k):
+        return pltpu.make_async_copy(edge_in.at[k], ein.at[k], l_edge.at[k])
+
+    def load_cot(k):
+        return pltpu.make_async_copy(cot_in.at[k], cn.at[k], l_cot.at[k])
+
+    def store_node(src, k):
+        return pltpu.make_async_copy(src.at[k], node_out.at[k], l_nout.at[k])
+
+    def store_edge(src, k):
+        return pltpu.make_async_copy(src.at[k], edge_out.at[k], l_eout.at[k])
+
+    def halo_copy(src, k, j, sems, segment):
+        rows = slice(j * HALO, (j + 1) * HALO)
+        into = slice(NODES_DEV + j * HALO, NODES_DEV + (j + 1) * HALO)
+        return remote(
+            src.at[k, rows], tab.at[k, into], sems.at[k, j], r_halo.at[k, j],
+            near(OFFSETS[j], segment),
+        )
+
+    def back_copy(dst, k, j, recv):
+        rows = slice(j * HALO, (j + 1) * HALO)
+        return remote(
+            bh.at[k, rows], dst.at[k, rows], s_bh.at[k, j], recv.at[k, j],
+            near(-OFFSETS[j], 0),
+        )
+
+    def sib_e(k):
+        return remote(enew.at[k], ein.at[k], s_fe.at[k], r_fe.at[k], {"segment": 1 - seg})
+
+    def sib_h(k):
+        return remote(
+            hnew.at[k], tab.at[k, 0:NODES_DEV], s_fh.at[k], r_fh.at[k], {"segment": 1 - seg}
+        )
+
+    def sib_de(k):
+        return remote(de.at[k], ce.at[k], s_be.at[k], r_be.at[k], {"segment": 1 - seg})
+
+    def sib_do(k):
+        return remote(down.at[k], cn32.at[k], s_bo.at[k], r_bo.at[k], {"segment": 1 - seg})
+
     large = [
         pltpu.make_async_copy(u.at[0], v, l_first.at[6 + i])
         for i, (u, v) in enumerate(
             [(w_ein_in, w_ein), (w_eout_in, w_eout), (w_nin_in, w_nin), (w_nout_in, w_nout)]
         )
     ]
-    for c in small:
-        c.start()
-
     @pl.when(first)
     def _():
         for k in range(2):
-            load_node(k).start()
             load_edge(k).start()
 
     @pl.when(second)
@@ -598,12 +602,9 @@
     for j, c in enumerate(flow_x):
         c.wait_recv()
         part = part + rx[j].astype(F4)
-    fin[16:32, LANES:] = part * factor
-    fin[0:16] = z_total(third_a, ca, ra)
-    fin[16:32, 0:LANES] = z_total(third_b, cb, rb)
-    result = pltpu.make_async_copy(fin, fin_out, l_fin.at[0])
-    result.start()
-    result.wait()
+    fin_out[16:32, LANES:] = part * factor
+    fin_out[0:16] = z_total(third_a, ca, ra)
+    fin_out[16:32, 0:LANES] = z_total(third_b, cb, rb)
     for c in ring_a.out + ring_b.out + second_a + second_b + third_a + third_b + flow_up + flow_low + flow_y + flow_x:
         c.wait_send()
 
@@ -648,12 +649,12 @@
     return pl.pallas_call(
         functools.partial(layer_kernel, nz=nz, factor=factor),
         out_shape=[
-            jax.ShapeDtypeStruct((2, n, 512), BF),
-            jax.ShapeDtypeStruct((2, e, 512), BF),
-            jax.ShapeDtypeStruct((32, 512), F4),
+            pltpu.VMEM((2, n, 512), BF),
+            pltpu.VMEM((2, e, 512), BF),
+            pltpu.VMEM((32, 512), F4),
         ],
         in_specs=[hbm] * 13,
-        out_specs=[hbm] * 3,
+        out_specs=[pl.BlockSpec(memory_space=pltpu.VMEM)] * 3,
         scratch_shapes=[
             pltpu.VMEM((e,), i32), pltpu.VMEM((e,), i32), pltpu.VMEM((1, 4, HALO), i32), pltpu.SMEM((1,), i32),
             bf(1536, 512), bf(512, 512), bf(1024, 512), bf(512, 512), fl(1, 512), fl(1, 512), dma((10,)),
@@ -674,10 +675,10 @@
             bf(4 * nz, 16, LANES), bf(4 * nz, 16, LANES), bf(4 * nz, 16, LANES),
             bf(4, nz, 16, 512), bf(3, nz, 16, 512),
             bf(4, nz, 16, LANES), bf(3, nz, 16, LANES),
-            bf(nz, 16, 512), bf(nz - 1, 16, 512), bf(nz, 16, LANES), bf(nz - 1, 16, LANES), fl(32, 512),
+            bf(nz, 16, 512), bf(nz - 1, 16, 512), bf(nz, 16, LANES), bf(nz - 1, 16, LANES),
             bf(nz, 4, 4, 16, 128), bf(4, 4, 4, 16, 128), bf(3, 4, 4, 16, 128),
             bf(4, 4, 16, 128), bf(3, 4, 16, 128), bf(4, 16, 128), bf(3, 16, 128),
-            dma((copies,)), dma((copies,)), dma((1,)),
+            dma((copies,)), dma((copies,)),
         ],
         compiler_params=pltpu.CompilerParams(
             collective_id=0, has_side_effects=True, vmem_limit_bytes=56 << 20
@@ -687,24 +688,14 @@
 
 
 def finish_kernel(
-    node_in, edge_in, fin_in, node_o, edge_o, ein_o, eout_o, nin_o, nout_o, ge_o, gn_o,
-    rfin, node_v, edge_v, sems, out_sems,
+    node_in, edge_in, rfin, node_o, edge_o, ein_o, eout_o, nin_o, nout_o, ge_o, gn_o, sems
 ):
-    first = pltpu.make_async_copy(fin_in, rfin, sems.at[0])
-    first.start()
-    parts = [(node_in.at[k], node_v.at[k], node_o.at[0, k]) for k in range(2)]
+    stores = []
     for k in range(2):
-        for q in range(2):
-            at = slice(q * 192, q * 192 + 192)
-            parts.append((edge_in.at[k, at], edge_v.at[k, at], edge_o.at[0, k, at]))
-    moves = [pltpu.make_async_copy(u, v, sems.at[1 + i]) for i, (u, v, _) in enumerate(parts)]
-    stores = [pltpu.make_async_copy(v, w, out_sems.at[i]) for i, (_, v, w) in enumerate(parts)]
-    for c in moves:
+        stores.append(pltpu.make_async_copy(edge_in.at[k], edge_o.at[0, k], sems.at[k]))
+        stores.append(pltpu.make_async_copy(node_in.at[k], node_o.at[0, k], sems.at[2 + k]))
+    for c in stores:
         c.start()
-    for c, w in zip(moves, stores):
-        c.wait()
-        w.start()
-    first.wait()
     t = lax.axis_index("dom") * 2 + lax.axis_index("rep")
     for r in range(12):
         ein_o[r] = rfin[r : r + 1]
@@ -739,13 +730,10 @@
             jax.ShapeDtypeStruct((1, 4), F4),
             jax.ShapeDtypeStruct((1, 4), F4),
         ],
-        in_specs=[hbm] * 3,
+        in_specs=[vm] * 3,
         out_specs=[hbm] * 2 + [vm] * 6,
-        scratch_shapes=[
-            pltpu.VMEM((32, 512), F4), pltpu.VMEM(node.shape, BF), pltpu.VMEM(edge.shape, BF),
-            pltpu.SemaphoreType.DMA((7,)), pltpu.SemaphoreType.DMA((6,)),
-        ],
-        compiler_params=pltpu.CompilerParams(vmem_limit_bytes=56 << 20),
+        scratch_shapes=[pltpu.SemaphoreType.DMA((4,))],
+        compiler_params=pltpu.CompilerParams(vmem_limit_bytes=16 << 20),
         name="finish",
     )(node, edge, fin)
 

time: 70.9 us -> 69.7 us (0.983)
  Pallas kernels: 68.3 us -> 67.5 us
    pallas_call x1, Pallas kernels: 2.73 us -> 1.63 us  [finish_call(): pl.pallas_call(finish_kernel, out_shape=[jax.ShapeDtypeStruct((1, *node.s...]
where the time goes in v7:
time: 69.7 us; the launch traced here: 68.8 us
  Pallas kernels  67.5 us (97%)
  between operations  1.29 us (2%)
    pallas_call x1, Pallas kernels, layer_call(): pl.pallas_call(functools.partial(layer_kernel, nz=nz, factor=factor), out...  65.8 us
    pallas_call x1, Pallas kernels, finish_call(): pl.pallas_call(finish_kernel, out_shape=[jax.ShapeDtypeStruct((1, *node.s...  1.63 us

profile of v7, /device:TPU:2, one launch (start us, length us, event | category | flops | bytes accessed | tf_op | source)
XLA Modules:
  0.0 68.8 jit_solution(12536612957219816196)
XLA Ops:
  1.3 65.8 %layers.1 = (bf16[2,128,512]{2,1,0:T(8,128)(2,1)S(1)}, bf16[2,384,512]{2,1,0:T(8,128)(2,1)S(1)}, f32[32,512]{1,0:T(8,128)S(1)}) custom-call(s32[384]{0:T(512)} %src_in.1, s32[384]{0:T(512)} %dst_in.1, s32[1,4,16]{2,1,0:T(4,128)} %send_in.1, s32[1]{0:T(128)S(6)} %copy.21.count_in, bf16[2,128,512]{2,1,0:T(8,128)(2,1)} %node_in.1, ...), custom_call_target="tpu_custom_call" | custom-call | tf_op jit(solution)/shard_map/layers/pallas_call | solution.py:649
  67.1 1.6 %finish.1 = (bf16[1,2,128,512]{3,2,1,0:T(8,128)(2,1)}, bf16[1,2,384,512]{3,2,1,0:T(8,128)(2,1)}, f32[12,1,512]{2,1,0:T(1,128)}, f32[1,4,512]{2,1,0:T(4,128)}, f3...) custom-call(bf16[2,128,512]{2,1,0:T(8,128)(2,1)S(1)} %get-tuple-element.19.node_in, ...), custom_call_target="tpu_custom_call" | custom-call | tf_op jit(solution)/shard_map/finish/pallas_call | solution.py:721

commit v8 on v7

--- a/solution.py
+++ b/solution.py
@@ -460,7 +460,11 @@
             self.me, self.right, self.left, self.cut = me, right, left, cut
 
         def start(self):
-            for c in self.out[:4]:
+            for c in self.out[:2]:
+                c.start()
+
+        def rest(self):
+            for c in self.out[2:4]:
                 c.start()
 
         def middle(self, block):
@@ -530,6 +534,7 @@
     gains = jnp.where(row == 0, sum_e, jnp.where(row == 1, sum_n, 0.0)).astype(BF)
     for q in range(4):
         ga[q, EDGES_DEV:, :] = gains
+    ring_b.rest()
     ring_a.start()
 
     @pl.when(first)
@@ -541,6 +546,7 @@
             store_node(dh, k).start()
 
     pass_on(0)
+    ring_a.rest()
     pass_on(1)
     ring_b.middle(2)
     ring_a.middle(16)

time: 69.7 us -> 70 us (level)
  no operation moved by 1% of the time
where the time goes in v8:
time: 70 us; the launch traced here: 68.8 us
  Pallas kernels  67.5 us (96%)
  between operations  1.29 us (2%)
    pallas_call x1, Pallas kernels, layer_call(): pl.pallas_call(functools.partial(layer_kernel, nz=nz, factor=factor), out...  65.8 us
    pallas_call x1, Pallas kernels, finish_call(): pl.pallas_call(finish_kernel, out_shape=[jax.ShapeDtypeStruct((1, *node.s...  1.63 us

profile of v8, /device:TPU:2, one launch (start us, length us, event | category | flops | bytes accessed | tf_op | source)
XLA Modules:
  0.0 68.8 jit_solution(14070836915389939951)
XLA Ops:
  1.3 65.8 %layers.1 = (bf16[2,128,512]{2,1,0:T(8,128)(2,1)S(1)}, bf16[2,384,512]{2,1,0:T(8,128)(2,1)S(1)}, f32[32,512]{1,0:T(8,128)S(1)}) custom-call(s32[384]{0:T(512)} %src_in.1, s32[384]{0:T(512)} %dst_in.1, s32[1,4,16]{2,1,0:T(4,128)} %send_in.1, s32[1]{0:T(128)S(6)} %copy.21.count_in, bf16[2,128,512]{2,1,0:T(8,128)(2,1)} %node_in.1, ...), custom_call_target="tpu_custom_call" | custom-call | tf_op jit(solution)/shard_map/layers/pallas_call | solution.py:655
  67.1 1.6 %finish.1 = (bf16[1,2,128,512]{3,2,1,0:T(8,128)(2,1)}, bf16[1,2,384,512]{3,2,1,0:T(8,128)(2,1)}, f32[12,1,512]{2,1,0:T(1,128)}, f32[1,4,512]{2,1,0:T(4,128)}, f3...) custom-call(bf16[2,128,512]{2,1,0:T(8,128)(2,1)S(1)} %get-tuple-element.19.node_in, ...), custom_call_target="tpu_custom_call" | custom-call | tf_op jit(solution)/shard_map/finish/pallas_call | solution.py:727
